TPU v7x, 32 devices: a whole 2x2x4 slice. The times are simulated.
32 devices in a mesh: fsdp: 4 (over y, x), seq: 8 (over z, core).
Axes of the slice: x: 2, y: 2, z: 4, core: 2. Of those that a mesh axis runs over, the one named last changes fastest.
Arguments:
- layer_input: bfloat16 [4, 1024, 1024], P('fsdp', 'seq'), may hold values from -6 to 6
- first_layer_values: bfloat16 [4, 1024, 1024], P('fsdp', 'seq'), may hold values from -6 to 6
- document_numbers: int32 [4, 1024], P('fsdp', 'seq'), may hold values from 0 to 1, as said below
- output_cotangent: bfloat16 [4, 1024, 1024], P('fsdp', 'seq'), may hold values from -6 to 6
- projection_matrices: bfloat16 [3, 1024, 1024], P(None, None, 'fsdp'), may hold values from -0.1875 to 0.1875
- time_output_matrix: bfloat16 [1024, 1024], P('fsdp'), may hold values from -0.25 to 0.25
- lowrank_first: bfloat16 [1024, 288], P('fsdp'), may hold values from -0.1875 to 0.1875
- lowrank_second: bfloat16 [288, 1024], P(None, 'fsdp'), may hold values from -0.75 to 0.75
- channel_key_matrix: bfloat16 [1024, 4096], P(None, 'fsdp'), may hold values from -0.1875 to 0.1875
- channel_value_matrix: bfloat16 [4096, 1024], P('fsdp'), may hold values from -0.09375 to 0.09375
- vectors: bfloat16 [19, 1024], P(None, 'fsdp'), may hold values from -8 to 2, as said below
Outputs:
- block_out: bfloat16 [4, 1024, 1024], P('fsdp', 'seq')
- d_input: float32 [4, 1024, 1024], P('fsdp', 'seq')
- d_v_first: float32 [4, 1024, 1024], P('fsdp', 'seq')
- grad_proj: float32 [3, 1024, 1024], P(None, None, 'fsdp')
- grad_out_weight: float32 [1024, 1024], P('fsdp')
- grad_lora_down: float32 [1024, 288], P('fsdp')
- grad_lora_up: float32 [288, 1024], P(None, 'fsdp')
- grad_key_weight: float32 [1024, 4096], P(None, 'fsdp')
- grad_value_weight: float32 [4096, 1024], P('fsdp')
- grad_vectors: float32 [19, 1024], P(None, 'fsdp')
Inputs may be any that keep to these rules, and one draw needn't show every extreme that they name: `document_numbers`: in each sequence the ids start at 0, never fall, rise by one at each new document and end at 1; every document holds 128 tokens or more. `vectors`: rows 0 to 5 and 18 lie in 0 to 1, row 6 in -8 to -1, rows 7 and 8 in -2 to 2, rows 9, 10, 12, 14, 16 in 0.5 to 1.5, row 11 in -0.25 to 0.25, rows 13, 15, 17 in -0.5 to 0.5.
All inputs are finite; a program needn't handle non-finite values.
Results may differ from a plain program's by a relative error of at most 0.024.
Values may be sent and summed in bfloat16 or wider, within the bound.
No kernel may reach another device: no remote copies, remote signals or barrier semaphores. Data moves between devices by JAX's collectives and lax.ppermute only.
A program may use at most 256 MiB of HBM per device.

v0:
```python
import jax
import jax.numpy as jnp
from jax import lax
from jax.sharding import PartitionSpec as P

ATTN_SLICE_SIZE = 64
DECAY_INNER = 64
RATE_INNER = 64
VALUE_MIX_INNER = 32
GATE_INNER = 128
SPAN = 32


LN_EPS = 1e-05
GROUP_EPS = 0.00064
UNIT_EPS = 1e-06


def shifted(value, axis, steps):
    count = lax.axis_size(axis)
    initial, last = (max(0, -steps), min(count, count - steps))
    return lax.ppermute(value, axis, [(source, source + steps) for source in range(initial, last)])


def shortened(array):
    return jax.tree.map(lambda a: a.astype(jnp.bfloat16) if a.dtype == jnp.float32 else a, array)


def matmul(left, right):
    return jnp.dot(left, right, preferred_element_type=jnp.float32)


def precise(pattern, left, right):
    return jnp.einsum(pattern, left, right, precision=lax.Precision.HIGHEST)


def layer_norm(values, gain, bias_row):
    center = values - jnp.mean(values, axis=-1, keepdims=True)
    spread = jnp.mean(center * center, axis=-1, keepdims=True)
    return center * lax.rsqrt(spread + LN_EPS) * gain + bias_row


def blend_rows(current, earlier, keep_row, gain_rows):
    change = earlier * keep_row - current
    return current[None] + change[None] * gain_rows[:, None, :]


def prepare(key_raw, value_raw, decay_up, alpha_up, vmix_up, first_value, vec_rows):
    line_total = key_raw.shape[0]
    w_log = -jax.nn.softplus(-(vec_rows[6] + decay_up)) - 0.5
    log_decay = -jnp.exp(w_log)
    alpha_gate = jax.nn.sigmoid(vec_rows[7] + alpha_up)
    value_gate = jax.nn.sigmoid(vec_rows[8] + vmix_up)
    merged_quantity = value_raw + (first_value - value_raw) * value_gate
    unit_key = (key_raw * vec_rows[9]).reshape(line_total, -1, ATTN_SLICE_SIZE)
    unit_key = unit_key * lax.rsqrt(jnp.sum(unit_key * unit_key, axis=-1, keepdims=True) + UNIT_EPS)
    unit_key = unit_key.reshape(line_total, -1)
    scaled_key = key_raw * (1.0 + (alpha_gate - 1.0) * vec_rows[10])
    return (log_decay, scaled_key, merged_quantity, -unit_key, unit_key * alpha_gate)


def finish(outputs, recept, scaled_key, merged_quantity, switch_raise_matrix, vec_rows):
    line_total = outputs.shape[0]
    grouped = outputs.reshape(line_total, -1, ATTN_SLICE_SIZE)
    center = grouped - jnp.mean(grouped, axis=-1, keepdims=True)
    spread = jnp.mean(center * center, axis=-1, keepdims=True)
    gaussian_sample = (center * lax.rsqrt(spread + GROUP_EPS)).reshape(line_total, -1) * vec_rows[
        12
    ] + vec_rows[13]
    extra_scaling = jnp.sum(
        (recept * scaled_key * vec_rows[11]).reshape(line_total, -1, ATTN_SLICE_SIZE),
        axis=-1,
        keepdims=True,
    )
    extra_term_result = (
        extra_scaling * merged_quantity.reshape(line_total, -1, ATTN_SLICE_SIZE)
    ).reshape(line_total, -1)
    return (gaussian_sample + extra_term_result) * switch_raise_matrix


def span_step(carried, pieces, same_doc, from_before):
    recept, log_decay, scaled_key, merged_quantity, a_vec, b_vec = pieces
    block_len = recept.shape[1]
    cumulative = jnp.cumsum(log_decay, axis=1)
    before = cumulative - log_decay
    total_log = cumulative[:, -1:, :]
    a_query = a_vec * jnp.exp(before)
    r_query = recept * jnp.exp(cumulative)
    b_keyed = b_vec * jnp.exp(-cumulative)
    k_keyed = scaled_key * jnp.exp(-cumulative)
    strict_mask = jnp.tril(jnp.ones((block_len, block_len), jnp.float32), -1) * same_doc
    incl_mask = jnp.tril(jnp.ones((block_len, block_len), jnp.float32)) * same_doc
    a_with_b = precise("htj,hsj->hts", a_query, b_keyed) * strict_mask
    a_with_k = precise("htj,hsj->hts", a_query, k_keyed) * strict_mask
    r_with_b = precise("htj,hsj->hts", r_query, b_keyed) * incl_mask
    r_with_k = precise("htj,hsj->hts", r_query, k_keyed) * incl_mask
    carried_in = from_before[:, :, None]
    right_side = precise("htj,hvj->htv", a_query * carried_in, carried) + precise(
        "hts,hsv->htv", a_with_k, merged_quantity
    )
    identity_mat = jnp.eye(block_len, dtype=jnp.float32)
    solved = jax.scipy.linalg.solve_triangular(
        identity_mat - a_with_b, right_side, lower=True, unit_diagonal=True
    )
    result_block = (
        precise("htj,hvj->htv", r_query * carried_in, carried)
        + precise("hts,hsv->htv", r_with_b, solved)
        + precise("hts,hsv->htv", r_with_k, merged_quantity)
    )
    tail_weight = jnp.exp(total_log - cumulative) * same_doc[:, -1][:, :, None]
    carried = (
        carried * (from_before[:, -1][:, None, None] * jnp.exp(total_log))
        + precise("hsv,hsj->hvj", solved, b_vec * tail_weight)
        + precise("hsv,hsj->hvj", merged_quantity, scaled_key * tail_weight)
    )
    return (result_block, carried)


def recurrence(carried, sources, same_docs, from_befores, groups, heads_here):
    line_total = sources[0].shape[0]
    blocks = same_docs.shape[0]
    span_len = same_docs.shape[-1]

    def by_heads(source):
        shaped = source.reshape(groups, blocks, span_len, heads_here, -1)
        return shaped.transpose(1, 0, 3, 2, 4).reshape(blocks, groups * heads_here, span_len, -1)

    split_rows = [by_heads(source) for source in sources]
    results = []
    for block_pos in range(blocks):
        pieces = tuple((source[block_pos] for source in split_rows))
        result_block, carried = span_step(
            carried, pieces, same_docs[block_pos], from_befores[block_pos]
        )
        results.append(result_block)
    joined = (
        jnp.stack(results)
        .reshape(blocks, groups, heads_here, span_len, -1)
        .transpose(1, 0, 3, 2, 4)
    )
    return (joined.reshape(line_total, heads_here, -1), carried)


def shift_up_local(source, incoming):
    return jnp.concatenate([source[1:], incoming])


def body(
    layer_input,
    first_layer_values,
    document_numbers,
    output_cotangent,
    projection_matrices,
    time_output_matrix,
    lowrank_first,
    lowrank_second,
    channel_key_matrix,
    channel_value_matrix,
    vectors,
):
    groups = lax.axis_size("fsdp")
    own_index = lax.axis_index("fsdp")
    small_parts = (
        lax.all_gather(lowrank_first, "fsdp", axis=0, tiled=True),
        lax.all_gather(vectors, "fsdp", axis=1, tiled=True),
    )
    down_complete, vector_full = small_parts
    wide_vec = vector_full.astype(jnp.float32)
    own_vec = vectors.astype(jnp.float32)
    lowrank_bounds = (
        0,
        DECAY_INNER,
        DECAY_INNER + RATE_INNER,
        DECAY_INNER + RATE_INNER + VALUE_MIX_INNER,
        DECAY_INNER + RATE_INNER + VALUE_MIX_INNER + GATE_INNER,
    )
    down_parts = [
        down_complete[:, lowrank_bounds[belongs] : lowrank_bounds[belongs + 1]]
        for belongs in range(4)
    ]
    second_parts = [
        lowrank_second[lowrank_bounds[belongs] : lowrank_bounds[belongs + 1]]
        for belongs in range(4)
    ]
    resid_in = layer_input[0].astype(jnp.float32)
    tokens_here = resid_in.shape[0]
    id_plus = document_numbers[0].astype(jnp.float32) + 1.0
    normed_one, ln_one_back = jax.vjp(layer_norm, resid_in, wide_vec[14], wide_vec[15])
    edge_row, edge_id = shifted(
        (normed_one[tokens_here - 1 :], id_plus[tokens_here - 1 :]), "seq", 1
    )
    earlier_ids = jnp.concatenate([edge_id, id_plus[:-1]])
    keep_flat = (id_plus == earlier_ids).astype(jnp.float32)
    keep_row = keep_flat[:, None]

    def mixer(current, earlier, gain_rows):
        return blend_rows(current, earlier, keep_row, gain_rows)

    earlier_one = jnp.concatenate([edge_row, normed_one[:-1]])
    mixed_rows, mix_back = jax.vjp(mixer, normed_one, earlier_one, wide_vec[0:6])
    mixed_b = mixed_rows.astype(jnp.bfloat16)
    decay_pre = matmul(mixed_b[1], down_parts[0])
    low_decay = jnp.tanh(decay_pre).astype(jnp.bfloat16)
    low_alpha = matmul(mixed_b[4], down_parts[1]).astype(jnp.bfloat16)
    low_vmix = matmul(mixed_b[3], down_parts[2]).astype(jnp.bfloat16)
    gate_pre = matmul(mixed_b[5], down_parts[3])
    low_gate = jax.nn.sigmoid(gate_pre).astype(jnp.bfloat16)
    lows_here = jnp.concatenate([low_decay, low_alpha, low_vmix, low_gate], axis=1)
    mix_three = jnp.stack([mixed_b[0], mixed_b[2], mixed_b[3]])
    gathered = (
        lax.all_gather(mix_three, "fsdp", axis=1, tiled=True),
        lax.all_gather(lows_here, "fsdp", axis=0, tiled=True),
        lax.all_gather(keep_row.astype(jnp.bfloat16), "fsdp", axis=0, tiled=True),
        lax.all_gather(output_cotangent[0], "fsdp", axis=0, tiled=True),
        lax.all_gather(first_layer_values[0], "fsdp", axis=0, tiled=True),
    )
    mix_rows, low_rows, keep_rows, cot_rows, first_rows = gathered
    width_here = projection_matrices.shape[2]
    heads_here = width_here // ATTN_SLICE_SIZE
    line_total = mix_rows.shape[1]
    first_cols = lax.dynamic_slice_in_dim(first_rows, own_index * width_here, width_here, 1).astype(
        jnp.float32
    )
    recept = matmul(mix_rows[0], projection_matrices[0])
    key_raw = matmul(mix_rows[1], projection_matrices[1])
    value_raw = matmul(mix_rows[2], projection_matrices[2])
    low_parts = [
        low_rows[:, lowrank_bounds[belongs] : lowrank_bounds[belongs + 1]] for belongs in range(4)
    ]
    decay_up = matmul(low_parts[0], second_parts[0])
    alpha_up = matmul(low_parts[1], second_parts[1])
    vmix_up = matmul(low_parts[2], second_parts[2])
    switch_raise_matrix = matmul(low_parts[3], second_parts[3])
    prepared, prep_back = jax.vjp(
        prepare, key_raw, value_raw, decay_up, alpha_up, vmix_up, first_cols, own_vec
    )
    log_decay, scaled_key, merged_quantity, a_vec, b_vec = prepared
    blocks = tokens_here // SPAN
    starts = 1.0 - keep_rows[:, 0].astype(jnp.float32)
    start_blocks = starts.reshape(groups, blocks, SPAN).transpose(1, 0, 2)
    segment = jnp.cumsum(start_blocks, axis=2)
    same_doc = (segment[:, :, :, None] == segment[:, :, None, :]).astype(jnp.float32)
    from_before = (segment == 0.0).astype(jnp.float32)
    batch_heads = groups * heads_here
    same_docs = jnp.broadcast_to(
        same_doc[:, :, None], (blocks, groups, heads_here, SPAN, SPAN)
    ).reshape(blocks, batch_heads, SPAN, SPAN)
    from_befores = jnp.broadcast_to(
        from_before[:, :, None], (blocks, groups, heads_here, SPAN)
    ).reshape(blocks, batch_heads, SPAN)
    eye_state = jnp.broadcast_to(
        jnp.eye(ATTN_SLICE_SIZE, dtype=jnp.float32), (batch_heads, ATTN_SLICE_SIZE, ATTN_SLICE_SIZE)
    )
    zero_state = jnp.zeros((batch_heads, ATTN_SLICE_SIZE, ATTN_SLICE_SIZE), jnp.float32)
    start_stacked = jnp.concatenate([eye_state, zero_state], axis=1)

    def local_wkv(recept_in, decay_in, key_in, value_in, avec_in, bvec_in):
        value_stacked = jnp.concatenate(
            [
                jnp.zeros((line_total, heads_here, ATTN_SLICE_SIZE), jnp.float32),
                value_in.reshape(line_total, heads_here, ATTN_SLICE_SIZE),
            ],
            axis=2,
        )
        joined, carried = recurrence(
            start_stacked,
            (recept_in, decay_in, key_in, value_stacked, avec_in, bvec_in),
            same_docs,
            from_befores,
            groups,
            heads_here,
        )
        return (
            joined[:, :, :ATTN_SLICE_SIZE],
            joined[:, :, ATTN_SLICE_SIZE:],
            carried[:, :ATTN_SLICE_SIZE],
            carried[:, ATTN_SLICE_SIZE:],
        )

    local_result, wkv_back = jax.vjp(
        local_wkv, recept, log_decay, scaled_key, merged_quantity, a_vec, b_vec
    )
    readout, outputs_zero, transfer, offset = local_result

    def forward_hop(step_no, incoming):
        leaving = precise("hvj,hjk->hvk", incoming, transfer) + offset
        return shifted(leaving, "seq", 1)

    state_in = lax.fori_loop(0, lax.axis_size("seq") - 1, forward_hop, zero_state)
    readout_four = readout.reshape(groups, tokens_here, heads_here, ATTN_SLICE_SIZE)
    state_four = state_in.reshape(groups, heads_here, ATTN_SLICE_SIZE, ATTN_SLICE_SIZE)
    carried_part = precise("nthj,nhvj->nthv", readout_four, state_four).reshape(
        line_total, heads_here, ATTN_SLICE_SIZE
    )
    outputs = (outputs_zero + carried_part).reshape(line_total, width_here)
    branch, fin_back = jax.vjp(
        finish, outputs, recept, scaled_key, merged_quantity, switch_raise_matrix, own_vec
    )
    branch_b = branch.astype(jnp.bfloat16)
    middle = resid_in + lax.psum_scatter(
        matmul(branch_b, time_output_matrix).astype(jnp.bfloat16),
        "fsdp",
        scatter_dimension=0,
        tiled=True,
    ).astype(jnp.float32)
    normed_two, ln_two_back = jax.vjp(layer_norm, middle, wide_vec[16], wide_vec[17])
    edge_two = shifted(normed_two[tokens_here - 1 :], "seq", 1)
    earlier_two = jnp.concatenate([edge_two, normed_two[:-1]])
    cmix_in, cmix_back = jax.vjp(mixer, normed_two, earlier_two, wide_vec[18:19])
    cmix_b = cmix_in[0].astype(jnp.bfloat16)
    cmix_rows = lax.all_gather(cmix_b, "fsdp", axis=0, tiled=True)
    pre_act = matmul(cmix_rows, channel_key_matrix)
    hidden_b = jnp.square(jax.nn.relu(pre_act)).astype(jnp.bfloat16)
    block_out = (
        middle
        + lax.psum_scatter(
            matmul(hidden_b, channel_value_matrix).astype(jnp.bfloat16),
            "fsdp",
            scatter_dimension=0,
            tiled=True,
        ).astype(jnp.float32)
    ).astype(jnp.bfloat16)
    grad_value = matmul(hidden_b.T, cot_rows)
    d_pre_b = (matmul(cot_rows, channel_value_matrix.T) * 2.0 * jax.nn.relu(pre_act)).astype(
        jnp.bfloat16
    )
    grad_key = matmul(cmix_rows.T, d_pre_b)
    d_cmix = lax.psum_scatter(
        matmul(d_pre_b, channel_key_matrix.T).astype(jnp.bfloat16),
        "fsdp",
        scatter_dimension=0,
        tiled=True,
    ).astype(jnp.float32)
    d_normed_two, d_earlier_two, d_cmix_gain = cmix_back(d_cmix[None])
    back_two = shifted(d_earlier_two[:1], "seq", -1)
    d_middle, d_gain_two, d_bias_two = ln_two_back(
        d_normed_two + shift_up_local(d_earlier_two, back_two)
    )
    d_middle = d_middle + output_cotangent[0].astype(jnp.float32)
    d_middle_b = d_middle.astype(jnp.bfloat16)
    dmid_rows = lax.all_gather(d_middle_b, "fsdp", axis=0, tiled=True)
    grad_out = matmul(branch_b.T, dmid_rows)
    d_branch = matmul(dmid_rows, time_output_matrix.T)
    d_outputs, d_recept_a, d_key_a, d_value_a, d_gate_up, d_vec_fin = fin_back(d_branch)
    d_out_four = d_outputs.reshape(groups, tokens_here, heads_here, ATTN_SLICE_SIZE)
    grad_start = precise("nthv,nthj->nhvj", d_out_four, readout_four).reshape(
        batch_heads, ATTN_SLICE_SIZE, ATTN_SLICE_SIZE
    )

    def backward_hop(step_no, incoming):
        leaving = precise("hvj,hkj->hvk", incoming, transfer) + grad_start
        return shifted(shortened(leaving), "seq", -1).astype(leaving.dtype)

    grad_end = lax.fori_loop(0, lax.axis_size("seq") - 1, backward_hop, zero_state)
    d_readout = precise("nthv,nhvj->nthj", d_out_four, state_four).reshape(
        line_total, heads_here, ATTN_SLICE_SIZE
    )
    d_transfer = precise("hvj,hvk->hjk", state_in, grad_end)
    wkv_grads = wkv_back(
        (
            d_readout,
            d_out_four.reshape(line_total, heads_here, ATTN_SLICE_SIZE),
            d_transfer,
            grad_end,
        )
    )
    d_recept_b, d_decay, d_key_b, d_value_b, d_avec, d_bvec = wkv_grads
    prep_grads = prep_back((d_decay, d_key_a + d_key_b, d_value_a + d_value_b, d_avec, d_bvec))
    d_key_raw, d_value_raw, d_decay_up, d_alpha_up, d_vmix_up, d_first_cols, d_vec_prep = prep_grads
    d_first_owner = lax.all_to_all(
        d_first_cols.astype(jnp.bfloat16), "fsdp", split_axis=0, concat_axis=1, tiled=True
    ).astype(d_first_cols.dtype)
    recept_g = (d_recept_a + d_recept_b).astype(jnp.bfloat16)
    key_g = d_key_raw.astype(jnp.bfloat16)
    value_g = d_value_raw.astype(jnp.bfloat16)
    decay_g = d_decay_up.astype(jnp.bfloat16)
    alpha_g = d_alpha_up.astype(jnp.bfloat16)
    vmix_g = d_vmix_up.astype(jnp.bfloat16)
    gate_g = d_gate_up.astype(jnp.bfloat16)
    grad_up = jnp.concatenate(
        [
            matmul(low_parts[0].T, decay_g),
            matmul(low_parts[1].T, alpha_g),
            matmul(low_parts[2].T, vmix_g),
            matmul(low_parts[3].T, gate_g),
        ],
        axis=0,
    )
    grad_proj = jnp.stack(
        [
            matmul(mix_rows[0].T, recept_g),
            matmul(mix_rows[1].T, key_g),
            matmul(mix_rows[2].T, value_g),
        ]
    )
    exchanged = lax.all_to_all(
        jnp.stack([recept_g, key_g, value_g, decay_g, alpha_g, vmix_g, gate_g]),
        "fsdp",
        split_axis=1,
        concat_axis=2,
        tiled=True,
    )
    wide_proj, wide_second = (
        lax.all_gather(projection_matrices, "fsdp", axis=2, tiled=True),
        lax.all_gather(lowrank_second, "fsdp", axis=1, tiled=True),
    )
    dmix_three = [matmul(exchanged[belongs], wide_proj[belongs].T) for belongs in range(3)]
    dlow_sum = jnp.concatenate(
        [
            matmul(
                exchanged[3 + belongs],
                wide_second[lowrank_bounds[belongs] : lowrank_bounds[belongs + 1]].T,
            )
            for belongs in range(4)
        ],
        axis=1,
    )
    tanh_now = jnp.tanh(decay_pre)
    low_decay_g = (
        dlow_sum[:, lowrank_bounds[0] : lowrank_bounds[1]] * (1.0 - tanh_now * tanh_now)
    ).astype(jnp.bfloat16)
    low_alpha_g = dlow_sum[:, lowrank_bounds[1] : lowrank_bounds[2]].astype(jnp.bfloat16)
    low_vmix_g = dlow_sum[:, lowrank_bounds[2] : lowrank_bounds[3]].astype(jnp.bfloat16)
    sigma_now = jax.nn.sigmoid(gate_pre)
    low_gate_g = (
        dlow_sum[:, lowrank_bounds[3] : lowrank_bounds[4]] * sigma_now * (1.0 - sigma_now)
    ).astype(jnp.bfloat16)
    grad_down = jnp.concatenate(
        [
            matmul(mixed_b[1].T, low_decay_g),
            matmul(mixed_b[4].T, low_alpha_g),
            matmul(mixed_b[3].T, low_vmix_g),
            matmul(mixed_b[5].T, low_gate_g),
        ],
        axis=1,
    )
    d_mixed = jnp.stack(
        [
            dmix_three[0],
            matmul(low_decay_g, down_parts[0].T),
            dmix_three[1],
            dmix_three[2] + matmul(low_vmix_g, down_parts[2].T),
            matmul(low_alpha_g, down_parts[1].T),
            matmul(low_gate_g, down_parts[3].T),
        ]
    )
    d_normed_one, d_earlier_one, d_mix_gains = mix_back(d_mixed)
    back_one = shifted(d_earlier_one[:1], "seq", -1)
    d_resid, d_gain_one, d_bias_one = ln_one_back(
        d_normed_one + shift_up_local(d_earlier_one, back_one)
    )
    d_input = d_resid + d_middle
    owner_vec = jnp.zeros((vector_full.shape[0], resid_in.shape[1]), jnp.float32)
    owner_vec = owner_vec.at[0:6].add(d_mix_gains).at[14].add(d_gain_one).at[15].add(d_bias_one)
    owner_vec = owner_vec.at[16].add(d_gain_two).at[17].add(d_bias_two).at[18].add(d_cmix_gain[0])
    down_owned, vec_owned = (
        lax.psum_scatter(
            grad_down.astype(jnp.bfloat16), "fsdp", scatter_dimension=0, tiled=True
        ).astype(jnp.float32),
        lax.psum_scatter(
            owner_vec.astype(jnp.bfloat16), "fsdp", scatter_dimension=1, tiled=True
        ).astype(jnp.float32),
    )
    vec_total = vec_owned + d_vec_fin + d_vec_prep
    summed = (
        lax.psum(grad_proj.astype(jnp.bfloat16), "seq").astype(jnp.float32),
        lax.psum(grad_out.astype(jnp.bfloat16), "seq").astype(jnp.float32),
        lax.psum(down_owned.astype(jnp.bfloat16), "seq").astype(jnp.float32),
        lax.psum(grad_up.astype(jnp.bfloat16), "seq").astype(jnp.float32),
        lax.psum(grad_key.astype(jnp.bfloat16), "seq").astype(jnp.float32),
        lax.psum(grad_value.astype(jnp.bfloat16), "seq").astype(jnp.float32),
        lax.psum(vec_total.astype(jnp.bfloat16), "seq").astype(jnp.float32),
    )
    return (
        block_out[None],
        d_input[None],
        d_first_owner[None],
        summed[0],
        summed[1],
        summed[2],
        summed[3],
        summed[4],
        summed[5],
        summed[6],
    )


def solution(mesh):
    in_specs = (
        P("fsdp", "seq", None),
        P("fsdp", "seq", None),
        P("fsdp", "seq"),
        P("fsdp", "seq", None),
        P(None, None, "fsdp"),
        P("fsdp", None),
        P("fsdp", None),
        P(None, "fsdp"),
        P(None, "fsdp"),
        P("fsdp", None),
        P(None, "fsdp"),
    )
    out_specs = (
        P("fsdp", "seq", None),
        P("fsdp", "seq", None),
        P("fsdp", "seq", None),
        P(None, None, "fsdp"),
        P("fsdp", None),
        P("fsdp", None),
        P(None, "fsdp"),
        P(None, "fsdp"),
        P("fsdp", None),
        P(None, "fsdp"),
    )
    return jax.shard_map(body, mesh=mesh, in_specs=in_specs, out_specs=out_specs, check_vma=False)
```

profile of v0, /device:TPU:0, one launch (start us, length us, event | category | flops | bytes accessed | tf_op | source)
XLA Modules:
  0.0 1192.4 jit_solution(544806653177922673)
XLA Ops:
  11.6 9.3 all_gather.33
  33.1 21.0 %all_gather.35 = bf16[1024,288]{0,1:T(8,128)(2,1)S(1)} all-gather(bf16[256,288]{0,1:T(8,128)(2,1)S(1)} %copy-done.295), channel_id=1, replica_groups=mesh['fsdp'=4,'seq'=8] {'fsdp'}, dimensions={0}, use_global_device_ids=true | all-gather | bytes 737280 | tf_op jit(solution)/shard_map/all_gather | solution.py:164
  71.4 10.4 all_gather.36
  141.8 41.0 %custom-call.15 = f32[16,1,32,32]{2,3,1,0:T(8,128)} custom-call(f32[16,1,32,32]{3,2,1,0:T(8,128)} %fusion.79), custom_call_target="InvertDiagBlocksLowerTriangular" | custom-call | tf_op jit(solution)/shard_map/jvp(jit(_solve_triangular))/vmap()/triangular_solve | solution.py:102
  195.9 40.8 %custom-call.16 = f32[16,1,32,32]{2,3,1,0:T(8,128)} custom-call(f32[16,1,32,32]{3,2,1,0:T(8,128)} %fusion.82), custom_call_target="InvertDiagBlocksLowerTriangular" | custom-call | tf_op jit(solution)/shard_map/jvp(jit(_solve_triangular))/vmap()/triangular_solve | solution.py:102
  250.1 41.2 %custom-call.17 = f32[16,1,32,32]{2,3,1,0:T(8,128)} custom-call(f32[16,1,32,32]{3,2,1,0:T(8,128)} %fusion.85), custom_call_target="InvertDiagBlocksLowerTriangular" | custom-call | tf_op jit(solution)/shard_map/jvp(jit(_solve_triangular))/vmap()/triangular_solve | solution.py:102
  319.7 40.9 %custom-call.18 = f32[16,1,32,32]{2,3,1,0:T(8,128)} custom-call(f32[16,1,32,32]{3,2,1,0:T(8,128)} %fusion.88), custom_call_target="InvertDiagBlocksLowerTriangular" | custom-call | tf_op jit(solution)/shard_map/jvp(jit(_solve_triangular))/vmap()/triangular_solve | solution.py:102
  382.3 86.0 %while.27 = (s32[]{:T(128)}, f32[16,64,64]{2,1,0:T(8,128)S(1)}, f32[16,64,64]{2,1,0:T(8,128)S(1)}, f32[16,64,64]{2,1,0:T(8,128)}, s32[]{:T(128)}) while((s32[]{:T(128)}, f32[16,64,64]{2,1,0:T(8,128)S(1)}, f32[16,64,64]{2,1,0:T(8,128)S(1)}, f32[16,64,64]{2,1,0:T(8,128)}, s32[]{:T(128)}) %tuple.265), condition=%wide.region_9.11_spmd, body=%wide.region_8.10_spmd.sunk | while | flops 50397184 | bytes 2097253 | solution.py:289
  390.3 10.4 collective-permute-start
  404.9 9.0 collective-permute-start
  418.1 9.0 collective-permute-start
  431.2 9.0 collective-permute-start
  485.6 34.5 %reduce-scatter.6.cloned.1.call-done = bf16[128,1024]{1,0:T(8,128)(2,1)} async-done(((bf16[512,1024]{1,0:T(8,128)(2,1)}), bf16[128,1024]{1,0:T(8,128)(2,1)}) %reduce-scatter.6.cloned.1.call-update) | async-done | bytes 262160 | tf_op jit(solution)/shard_map/reduce_scatter | solution.py:300
  528.5 28.6 %all-gather.11.cloned.1.call-done = bf16[512,1024]{1,0:T(8,128)(2,1)} async-done(((bf16[128,1024]{1,0:T(8,128)(2,1)}), bf16[512,1024]{1,0:T(8,128)(2,1)}) %all-gather.11.cloned.1.call-update) | async-done | bytes 1048592 | tf_op jit(solution)/shard_map/all_gather | solution.py:311
  560.9 24.4 %all-gather.19.cloned.1.call-done = bf16[1,512,1024]{2,1,0:T(8,128)(2,1)} async-done(((bf16[1,128,1024]{2,1,0:T(8,128)(2,1)}), bf16[1,512,1024]{2,1,0:T(8,128)(2,1)}) %all-gather.19.cloned.1.call-update) | async-done | bytes 1048592 | tf_op jit(solution)/shard_map/all_gather | solution.py:214
  597.0 23.5 %reduce-scatter.10.cloned.1.call-done = bf16[128,1024]{1,0:T(8,128)(2,1)} async-done(((bf16[512,1024]{1,0:T(8,128)(2,1)}), bf16[128,1024]{1,0:T(8,128)(2,1)}) %reduce-scatter.10.cloned.1.call-update) | async-done | bytes 262160 | tf_op jit(solution)/shard_map/reduce_scatter | solution.py:328
  626.8 25.2 %reduce-scatter.8.cloned.1.call-done = bf16[128,1024]{1,0:T(8,128)(2,1)} async-done(((bf16[512,1024]{1,0:T(8,128)(2,1)}), bf16[128,1024]{1,0:T(8,128)(2,1)}) %reduce-scatter.8.cloned.1.call-update) | async-done | bytes 262160 | tf_op jit(solution)/shard_map/reduce_scatter | solution.py:316
  655.6 17.6 %all_gather.43 = bf16[288,1024]{1,0:T(8,128)(2,1)} all-gather(bf16[288,256]{1,0:T(8,128)(2,1)S(1)} %copy-done.281), channel_id=1, replica_groups=mesh['fsdp'=4,'seq'=8] {'fsdp'}, dimensions={1}, use_global_device_ids=true | all-gather | bytes 737280 | tf_op jit(solution)/shard_map/all_gather | solution.py:405
  701.2 58.5 %while.28 = (s32[]{:T(128)}, f32[16,64,64]{2,1,0:T(8,128)S(1)}, f32[16,64,64]{2,1,0:T(8,128)S(1)}, f32[16,64,64]{2,1,0:T(8,128)S(1)}, s32[]{:T(128)}, /*index=5*/s32[]{:T(128)}) while((s32[]{:T(128)}, f32[16,64,64]{2,1,0:T(8,128)S(1)}, f32[16,64,64]{2,1,0:T(8,128)S(1)}, f32[16,64,64]{2,1,0:T(8,128)S(1)}, s32[]{:T(128)}, ...), condition=%wide.region_24.26_spmd.clone, body=%wide.region_23.25_spmd.clone.sunk | while | flops 50593792 | bytes 1835127 | solution.py:354
  914.5 13.9 %all-to-all-done = bf16[7,512,256]{2,0,1:T(8,128)(2,1)S(1)} async-done(((bf16[7,512,256]{2,0,1:T(8,128)(2,1)}), bf16[7,512,256]{2,0,1:T(8,128)(2,1)S(1)}, u32[]{:S(2)}, u32[]{:S(2)}) %all-to-all-start) | async-done | bytes 1835040 | tf_op jit(solution)/shard_map/all_to_all | solution.py:396
  980.2 21.0 %reduce-scatter.12.cloned.1.call-done = bf16[256,288]{0,1:T(8,128)(2,1)} async-done(((bf16[1024,288]{0,1:T(8,128)(2,1)}), bf16[256,288]{0,1:T(8,128)(2,1)}) %reduce-scatter.12.cloned.1.call-update) | async-done | bytes 147472 | tf_op jit(solution)/shard_map/reduce_scatter | solution.py:457
  1013.0 15.1 %reduce-scatter.14.cloned.1.call-done = bf16[19,256]{1,0:T(8,128)(2,1)} async-done(((bf16[19,1024]{1,0:T(8,128)(2,1)}), bf16[19,256]{1,0:T(8,128)(2,1)}) %reduce-scatter.14.cloned.1.call-update) | async-done | bytes 9744 | tf_op jit(solution)/shard_map/reduce_scatter | solution.py:460
  1028.8 29.3 %psum.55 = bf16[19,256]{1,0:T(8,128)(2,1)S(1)} all-reduce(bf16[19,256]{1,0:T(8,128)(2,1)S(1)} %add_convert_fusion.6), channel_id=1, replica_groups=mesh['fsdp'=4,'seq'=8] {'seq'}, use_global_device_ids=true, to_apply=%region_63.66 | all-reduce | flops 4864 | bytes 19456 | tf_op jit(solution)/shard_map/psum | solution.py:472
  1058.7 115.7 %all-reduce.46.cloned.1.call-done = (bf16[3,1024,256]{2,1,0:T(8,128)(2,1)}, bf16[256,1024]{1,0:T(8,128)(2,1)}, bf16[256,288]{0,1:T(8,128)(2,1)}, bf16[288,256]{1...) async-done(((bf16[3,1024,256]{2,1,0:T(8,128)(2,1)}, bf16[256,1024]{1,0:T(8,128)(2,1)}, bf16[256,288]{0,1:T(8,128)(2,1)}, ...) | async-done | bytes 6586384 | tf_op jit(solution)/shard_map/psum | solution.py:466
  (1266 shorter events, 580.9 us)
Async XLA Ops:
  7.2 88.0 %all-gather.9.cloned.1.call-start = ((), (), s32[]{:S(2)}) async-start(), calls=%async_computation.7 | async-start | bytes 3932160 | tf_op jit(solution)/shard_map/all_gather | solution.py:211
  8.7 18.2 %collective-permute-start.3 = (f32[1]{0:T(128)}, f32[1]{0:T(128)}, u32[]{:S(2)}, u32[]{:S(2)}) collective-permute-start(f32[1]{0:T(128)} %bitcast.7), channel_id=1, source_target_pairs={{0,1},{1,2},{2,3},{3,4},{4,5},{5,6},{6,7},{8,9},{9,10},{10,11},{11... | collective-permute-start | bytes 20 | tf_op jit(solution)/shard_map/ppermute | solution.py:22
  30.7 99.8 %all-gather.17.cloned.1.call-start = ((), (), s32[]{:S(2)}) async-start(), calls=%async_computation.16 | async-start | bytes 1310720 | tf_op jit(solution)/shard_map/all_gather | solution.py:215
  31.7 488.4 %reduce-scatter.6.cloned.1.call-start = ((), (), s32[]{:S(2)}) async-start(), calls=%async_computation.8 | async-start | bytes 1310720 | tf_op jit(solution)/shard_map/reduce_scatter | solution.py:300
  390.3 12.1 %collective-permute-start = (f32[16,64,64]{2,1,0:T(8,128)}, f32[16,64,64]{2,1,0:T(8,128)S(1)}, u32[]{:S(2)}, u32[]{:S(2)}) collective-permute-start(f32[16,64,64]{2,1,0:T(8,128)} %convolution_add_fusion.62), channel_id=1, source_target_pairs={{0,1},{1,2},{2,3},{3,4},{4,5},{5,6},{6,7},{8,9},{9,10},{10,11},{11... | collective-permute-start | bytes 786440 | tf_op jit(solution)/shard_map/while/body/eval_jaxpr/ppermute | solution.py:22
  404.9 10.7 collective-permute-start
  418.1 10.7 collective-permute-start
  431.2 10.7 collective-permute-start
  444.4 10.7 collective-permute-start
  457.6 10.7 collective-permute-start
  485.1 72.0 %all-gather.11.cloned.1.call-start = ((), (), s32[]{:S(2)}) async-start(), calls=%async_computation.9 | async-start | bytes 1310720 | tf_op jit(solution)/shard_map/all_gather | solution.py:311
  527.9 57.4 %all-gather.19.cloned.1.call-start = ((), (), s32[]{:S(2)}) async-start(), calls=%async_computation.17 | async-start | bytes 1310720 | tf_op jit(solution)/shard_map/all_gather | solution.py:214
  528.5 92.0 %reduce-scatter.10.cloned.1.call-start = ((), (), s32[]{:S(2)}) async-start(), calls=%async_computation.11 | async-start | bytes 1310720 | tf_op jit(solution)/shard_map/reduce_scatter | solution.py:328
  592.4 59.5 %reduce-scatter.8.cloned.1.call-start = ((), (), s32[]{:S(2)}) async-start(), calls=%async_computation.10 | async-start | bytes 1310720 | tf_op jit(solution)/shard_map/reduce_scatter | solution.py:316
  597.0 87.3 %all-gather.13.cloned.1.call-start = ((), (), s32[]{:S(2)}) async-start(), calls=%async_computation.12 | async-start | bytes 1310720 | tf_op jit(solution)/shard_map/all_gather | solution.py:341
  654.8 280.0 %all-gather.15.cloned.1.call-start = ((), (), s32[]{:S(2)}) async-start(), calls=%async_computation.13 | async-start | bytes 7864320 | tf_op jit(solution)/shard_map/all_gather | solution.py:404
  724.0 8.1 collective-permute-start.1
  733.1 8.1 collective-permute-start.1
  751.4 8.1 collective-permute-start.1
  899.6 28.8 %all-to-all-start = ((bf16[7,512,256]{2,0,1:T(8,128)(2,1)}), bf16[7,512,256]{2,0,1:T(8,128)(2,1)S(1)}, u32[]{:S(2)}, u32[]{:S(2)}) async-start(bf16[7,512,256]{2,0,1:T(8,128)(2,1)} %copy.731), calls=%async_computation.3 | async-start | bytes 4194304 | tf_op jit(solution)/shard_map/all_to_all | solution.py:396
  903.2 98.0 %reduce-scatter.12.cloned.1.call-start = ((), (), s32[]{:S(2)}) async-start(), calls=%async_computation.14 | async-start | bytes 737280 | tf_op jit(solution)/shard_map/reduce_scatter | solution.py:457
  971.1 57.0 %reduce-scatter.14.cloned.1.call-start = ((), (), s32[]{:S(2)}) async-start(), calls=%async_computation.15 | async-start | bytes 61440 | tf_op jit(solution)/shard_map/reduce_scatter | solution.py:460
  978.6 195.8 %all-reduce.46.cloned.1.call-start = ((), (), s32[]{:S(2)}) async-start(), calls=%async_computation.18 | async-start | bytes 13172736 | tf_op jit(solution)/shard_map/psum | solution.py:466
  1002.1 8.8 all-to-all-start.1
  (375 other events, 3160.6 us)
Sparse Core Ops, SparseCore 0:
  30.8 52.9 all-gather.8
  86.2 26.2 all-gather.16
  485.2 34.8 reduce-scatter.5
  528.0 29.0 all-gather.10
  558.8 26.4 all-gather.18
  592.6 27.9 reduce-scatter.9
  624.0 27.9 reduce-scatter.7
  654.9 29.2 all-gather.12
  686.1 69.8 all-gather.14
  971.2 30.0 reduce-scatter.11
  1004.5 23.4 reduce-scatter.13
  1031.9 142.4 all-reduce.45
where the time goes:
time: 1200 us; the launch traced here: 1190 us
  waiting for transfers between devices  369 us (31%)
  other arithmetic  258 us (22%)
  matrix products  225 us (19%)
  local copies, waits for them, and re-layouts  140 us (12%)
  blocking collectives  96.4 us (8%)
  starting transfers between devices  82.7 us (7%)
  between operations  20.2 us (2%)
    another operation x7, other arithmetic, span_step(): jax.scipy.linalg.solve_triangular(identity_mat - a_with_b, right_side, lo...  164 us
    dot_general x148, matrix products, precise(): return jnp.einsum(pattern, left, right, precision=lax.Precision.HIGHEST)  140 us
    psum x1, waiting for transfers between devices, body(): lax.psum(grad_proj.astype(jnp.bfloat16), 'seq').astype(jnp.float32)  116 us
    dot_general x42, matrix products, matmul(): return jnp.dot(left, right, preferred_element_type=jnp.float32)  76.6 us
    ppermute x19, starting transfers between devices, shifted(): lax.ppermute(value, axis, [(source, source + steps) for source in range(i...  74.7 us
    ppermute x19, waiting for transfers between devices, shifted(): lax.ppermute(value, axis, [(source, source + steps) for source in range(i...  56.2 us
    reduce_scatter x1, waiting for transfers between devices, body(): lax.psum_scatter(matmul(branch_b, time_output_matrix).astype(jnp.bfloat16...  34.5 us
    psum x1, blocking collectives, body(): lax.psum(vec_total.astype(jnp.bfloat16), 'seq').astype(jnp.float32)  29.3 us
  transfers between devices with their start and end apart: 33, of which 27 were waited for; matrix products, arithmetic and copies ran while one was open for 23% of the time, Pallas kernels for 0%

commit v1 on v0

v1 whole, which is shorter than its diff:
```python
import jax
import jax.numpy as jnp
from jax import lax
from jax.experimental import pallas as pl
from jax.experimental.pallas import tpu as pltpu
from jax.sharding import PartitionSpec as P

F32 = jnp.float32
BF16 = jnp.bfloat16
HEAD = 64
PAIR = 128
BOUNDS = (0, 64, 128, 160, 288)
LN_EPS = 1e-05
GROUP_EPS = 0.00064
UNIT_EPS = 1e-06
NN = (((1,), (0,)), ((), ()))
NT = (((1,), (1,)), ((), ()))
TN = (((0,), (0,)), ((), ()))


def mm(left, right, dims=NN):
    return lax.dot_general(
        left.astype(BF16), right.astype(BF16), dims, preferred_element_type=F32
    )


def mm_exact_left(left, right, dims=NN):
    high = right.astype(BF16)
    low = (right - high.astype(F32)).astype(BF16)
    return lax.dot_general(left, high, dims, preferred_element_type=F32) + lax.dot_general(
        left, low, dims, preferred_element_type=F32
    )


def mm_exact_right(left, right):
    high = left.astype(BF16)
    low = (left - high.astype(F32)).astype(BF16)
    return lax.dot_general(high, right, NN, preferred_element_type=F32) + lax.dot_general(
        low, right, NN, preferred_element_type=F32
    )


def lane_halves(shape):
    lane = lax.broadcasted_iota(jnp.int32, shape, 1)
    return lane < HEAD


def halves(array):
    first = lane_halves(array.shape)
    zero = jnp.zeros_like(array)
    return (jnp.where(first, array, zero), jnp.where(first, zero, array))


def head_sums(array):
    row = lax.broadcasted_iota(jnp.int32, (PAIR, PAIR), 0)
    col = lax.broadcasted_iota(jnp.int32, (PAIR, PAIR), 1)
    ones = jnp.where((row < HEAD) == (col < HEAD), 1.0, 0.0).astype(BF16)
    return mm_exact_right(array, ones)


def compact(block):
    return jnp.where(lane_halves((HEAD, PAIR)), block[:HEAD], block[HEAD:])


def spread(pair):
    return jnp.concatenate(halves(pair), axis=0)


def prepared(kr, vr, du, au, vu, fv, vec):
    decay_in = vec[6:7] + du
    sig = jax.nn.sigmoid(decay_in)
    ld = sig * (-0.6065306597126334)
    alpha = jax.nn.sigmoid(vec[7:8] + au)
    vg = jax.nn.sigmoid(vec[8:9] + vu)
    mv = vr + (fv - vr) * vg
    raw_unit = kr * vec[9:10]
    scale = lax.rsqrt(head_sums(raw_unit * raw_unit) + UNIT_EPS)
    unit = raw_unit * scale
    mult = 1.0 + (alpha - 1.0) * vec[10:11]
    sk = kr * mult
    return (sig, ld, alpha, vg, mv, scale, unit, mult, sk)


def scaled_parts(r, ld, sk, unit, alpha, seg_col, seg_row):
    span = r.shape[0]
    row = lax.broadcasted_iota(jnp.int32, (span, span), 0)
    col = lax.broadcasted_iota(jnp.int32, (span, span), 1)
    tril = jnp.where(row >= col, 1.0, 0.0).astype(BF16)
    cum = mm_exact_left(tril, ld)
    mid = cum[span // 2 - 1 : span // 2]
    end = cum[span - 1 : span]
    ea = jnp.exp(cum - ld - mid)
    er = jnp.exp(cum - mid)
    eb = jnp.exp(mid - cum)
    at = -unit * ea
    rt = r * er
    bt = unit * alpha * eb
    kt = sk * eb
    fresh = jnp.where(seg_col == 0.0, 1.0, 0.0)
    lead = jnp.exp(mid) * fresh
    tail = jnp.exp(end - mid) * jnp.where(seg_col == seg_col[span - 1 : span], 1.0, 0.0)
    through = jnp.exp(end) * fresh[span - 1 : span]
    same = seg_col[:, :span] == seg_row
    strict = same & (row > col)
    incl = same & (row >= col)
    return (at, rt, bt, kt, ea, er, eb, lead, tail, through, strict, incl)


def split_terms(array):
    high = array.astype(BF16)
    return (high, (array - high.astype(F32)).astype(BF16))


def interactions(at, rt, bt, kt, strict, incl):
    span = at.shape[0]
    left_high, left_low = split_terms(jnp.concatenate([at, rt], axis=0))
    right_high, right_low = split_terms(jnp.concatenate([bt, kt], axis=0))
    left_high = halves(left_high)
    left_low = halves(left_low)
    right = jnp.concatenate([right_high, right_high, right_low], axis=1)
    result = []
    for half in range(2):
        left = jnp.concatenate([left_high[half], left_low[half], left_high[half]], axis=1)
        full = mm(left, right, NT)
        result.append(
            (
                jnp.where(strict, full[:span, :span], 0.0),
                jnp.where(strict, full[:span, span:], 0.0),
                jnp.where(incl, full[span:, :span], 0.0),
                jnp.where(incl, full[span:, span:], 0.0),
            )
        )
    return result


def unit_inverse(lower):
    span = lower.shape[0]
    row = lax.broadcasted_iota(jnp.int32, (span, span), 0)
    col = lax.broadcasted_iota(jnp.int32, (span, span), 1)
    size = 1
    differ = row ^ col
    solved = jnp.where(row == col, 1.0, 0.0) + jnp.where(differ == 1, lower, 0.0)
    size = 2
    while size < span:
        part = jnp.where((differ >= size) & (differ < 2 * size), lower, 0.0)
        solved = solved + mm(solved, mm(part, solved))
        size *= 2
    return solved


def forward_body(
    r_ref, kr_ref, vr_ref, du_ref, au_ref, vu_ref, fv_ref, vec_ref, seg_col_ref, seg_row_ref,
    q_ref, y_ref, u0_ref, out_ref, bonus_ref, x_ref, t_ref, o_ref,
):
    vec = vec_ref[...]
    r = r_ref[...]
    sig, ld, alpha, vg, mv, scale, unit, mult, sk = prepared(
        kr_ref[...], vr_ref[...], du_ref[...], au_ref[...], vu_ref[...],
        fv_ref[...].astype(F32), vec,
    )
    at, rt, bt, kt, ea, er, eb, lead, tail, through, strict, incl = scaled_parts(
        r, ld, sk, unit, alpha, seg_col_ref[...], seg_row_ref[0:1]
    )
    span = r.shape[0]
    inter = interactions(at, rt, bt, kt, strict, incl)
    inverse = [unit_inverse(inter[half][0]) for half in range(2)]
    v_half = [part.astype(BF16) for part in halves(mv)]
    av = mm(
        jnp.concatenate([inter[0][1], inter[1][1]], axis=1),
        jnp.concatenate(v_half, axis=0),
    )
    a_in = at * lead
    right = jnp.concatenate([av, a_in], axis=1)
    first = lax.broadcasted_iota(jnp.int32, right.shape, 1) % PAIR < HEAD
    solved = mm(
        jnp.concatenate(inverse, axis=1),
        jnp.concatenate([jnp.where(first, right, 0.0), jnp.where(first, 0.0, right)], axis=0),
    )
    u0 = solved[:, :PAIR]
    y = solved[:, PAIR:]
    uy = solved.astype(BF16)
    zero = jnp.zeros_like(uy)
    zero_half = jnp.zeros_like(v_half[0])
    joined = mm(
        jnp.concatenate([inter[0][2], inter[1][2], inter[0][3], inter[1][3]], axis=1),
        jnp.concatenate(
            [
                jnp.where(first, uy, zero),
                jnp.where(first, zero, uy),
                jnp.concatenate([v_half[0], zero_half], axis=1),
                jnp.concatenate([v_half[1], zero_half], axis=1),
            ],
            axis=0,
        ),
    )
    q_ref[...] = (rt * lead + joined[:, PAIR:]).astype(q_ref.dtype)
    out_ref[...] = joined[:, :PAIR]
    y_ref[...] = y.astype(y_ref.dtype)
    u0_ref[...] = u0
    b_tail = bt * tail
    k_tail = kt * tail
    diag_row = lax.broadcasted_iota(jnp.int32, (PAIR, PAIR), 0)
    diag_col = lax.broadcasted_iota(jnp.int32, (PAIR, PAIR), 1)
    transfer = mm(y, b_tail, TN) + jnp.where(diag_row == diag_col, through, 0.0)
    offset = mm(
        jnp.concatenate([u0, mv], axis=0), jnp.concatenate([b_tail, k_tail], axis=0), TN
    )
    t_ref[0] = compact(transfer)
    o_ref[0] = compact(offset)
    x_ref[0] = jnp.concatenate(inverse, axis=0).astype(x_ref.dtype)
    bonus_ref[...] = head_sums(r * sk * vec[11:12]) * mv


def finish_body(q_ref, out_ref, bonus_ref, s_ref, gate_ref, vec_ref, xhat_ref, rstd_ref, branch_ref):
    vec = vec_ref[...]
    out = out_ref[...] + mm(q_ref[...], spread(s_ref[0]), NT)
    center = out - head_sums(out) * (1.0 / HEAD)
    rstd = lax.rsqrt(head_sums(center * center) * (1.0 / HEAD) + GROUP_EPS)
    xhat = center * rstd
    xhat_ref[...] = xhat
    rstd_ref[...] = rstd
    branch_ref[...] = (
        (xhat * vec[12:13] + vec[13:14] + bonus_ref[...]) * gate_ref[...]
    ).astype(branch_ref.dtype)


def early_body(
    db_ref, gate_ref, xhat_ref, rstd_ref, bonus_ref, q_ref, vec_ref,
    dout_ref, dbg_ref, dgate_ref, gs_ref, gvec_ref,
):
    vec = vec_ref[...]
    d_branch = db_ref[...]
    xhat = xhat_ref[...]
    inner = xhat * vec[12:13] + vec[13:14] + bonus_ref[...]
    dgate_ref[...] = (d_branch * inner).astype(dgate_ref.dtype)
    dbg = d_branch * gate_ref[...]
    dbg_ref[...] = dbg
    dn = dbg * vec[12:13]
    dout = rstd_ref[...] * (
        dn - head_sums(dn) * (1.0 / HEAD) - xhat * (head_sums(dn * xhat) * (1.0 / HEAD))
    )
    dout_ref[...] = dout
    gs_ref[0] = compact(mm(dout, q_ref[...], TN))
    gvec_ref[...] = jnp.zeros_like(gvec_ref)
    gvec_ref[4:5] = jnp.sum(dbg * xhat, axis=0, keepdims=True)
    gvec_ref[5:6] = jnp.sum(dbg, axis=0, keepdims=True)


def late_body(
    r_ref, kr_ref, vr_ref, du_ref, au_ref, vu_ref, fv_ref, vec_ref, seg_col_ref, seg_row_ref,
    x_ref, y_ref, u0_ref, s_ref, g_ref, dout_ref, dbg_ref,
    dr_out, dk_out, dv_out, ddu_out, dau_out, dvu_out, dfv_out, gvec_ref,
):
    vec = vec_ref[...]
    r = r_ref[...]
    kr = kr_ref[...]
    vr = vr_ref[...]
    fv = fv_ref[...].astype(F32)
    sig, ld, alpha, vg, mv, scale, unit, mult, sk = prepared(
        kr, vr, du_ref[...], au_ref[...], vu_ref[...], fv, vec
    )
    at, rt, bt, kt, ea, er, eb, lead, tail, through, strict, incl = scaled_parts(
        r, ld, sk, unit, alpha, seg_col_ref[...], seg_row_ref[0:1]
    )
    span = r.shape[0]
    inter = interactions(at, rt, bt, kt, strict, incl)
    state = spread(s_ref[0])
    grad = spread(g_ref[0])
    u = u0_ref[...] + mm(y_ref[...], state, NT)
    dout = dout_ref[...]
    dout_half = [part.astype(BF16) for part in halves(dout)]
    first_pass = mm(
        jnp.concatenate(
            [
                jnp.concatenate([inter[0][2], inter[0][3]], axis=1),
                jnp.concatenate([inter[1][2], inter[1][3]], axis=1),
            ],
            axis=0,
        ),
        jnp.concatenate(dout_half, axis=0),
        TN,
    )
    b_tail = bt * tail
    k_tail = kt * tail
    from_grad = mm(jnp.concatenate([b_tail, k_tail], axis=0), grad, NT)
    first_pass = first_pass + from_grad
    d_u = first_pass[:span]
    d_mv = first_pass[span:]
    w = mm(x_ref[0], jnp.concatenate(halves(d_u), axis=0), TN)
    w_half = [part.astype(BF16) for part in halves(w)]
    d_mv = d_mv + mm(
        jnp.concatenate([inter[0][1], inter[1][1]], axis=0),
        jnp.concatenate(w_half, axis=0),
        TN,
    )
    uv = jnp.concatenate([u, mv], axis=0).astype(BF16)
    bk = jnp.concatenate([bt, kt], axis=0)
    ar = jnp.concatenate([at, rt], axis=0)
    bk_half = halves(bk)
    ar_half = halves(ar)
    d_inter = []
    mask = jnp.concatenate([strict, strict], axis=1)
    mask = jnp.concatenate([mask, mask], axis=0)
    for half in range(2):
        full = mm(jnp.concatenate([w_half[half], dout_half[half]], axis=0), uv, NT)
        d_inter.append(jnp.where(mask, full, 0.0).astype(BF16))
    diag_b = head_sums(dout * u)
    diag_k = head_sums(dout * mv)
    d_ar = mm(jnp.concatenate(d_inter, axis=1), jnp.concatenate(bk_half, axis=0))
    d_bk = mm(jnp.concatenate(d_inter, axis=0), jnp.concatenate(ar_half, axis=0), TN)
    wd = jnp.concatenate([w, dout], axis=0)
    d_in = mm(wd, state)
    d_tail = mm(uv, grad)
    d_at = d_ar[:span] + d_in[:span] * lead
    d_rt = d_ar[span:] + d_in[span:] * lead
    d_bt = d_bk[:span] + d_tail[:span] * tail
    d_kt = d_bk[span:] + d_tail[span:] * tail
    d_before = at * d_at
    d_cum = rt * d_rt - bt * d_bt - kt * d_kt
    at_end = jnp.sum(b_tail * d_tail[:span] + k_tail * d_tail[span:], axis=0, keepdims=True)
    at_end = at_end + through * jnp.sum(s_ref[0] * g_ref[0], axis=0, keepdims=True)
    row = lax.broadcasted_iota(jnp.int32, (span, span), 0)
    col = lax.broadcasted_iota(jnp.int32, (span, span), 1)
    triu = jnp.where(row <= col, 1.0, 0.0).astype(BF16)
    d_ld = mm_exact_left(triu, d_cum + d_before) - d_before + at_end
    d_r = d_rt * er + diag_b * (unit * alpha) + diag_k * sk
    d_a = d_at * ea
    d_b = d_bt * eb + diag_b * r
    d_sk = d_kt * eb + diag_k * r
    dbg = dbg_ref[...]
    extra = head_sums(r * sk * vec[11:12])
    d_extra = head_sums(dbg * mv)
    d_mv = d_mv + dbg * extra
    d_r = d_r + d_extra * sk * vec[11:12]
    d_sk = d_sk + d_extra * r * vec[11:12]
    d_unit = d_b * alpha - d_a
    d_alpha = d_b * unit + d_sk * kr * vec[10:11]
    d_raw = scale * (d_unit - unit * head_sums(d_unit * unit))
    d_kr = d_raw * vec[9:10] + d_sk * mult
    d_du = d_ld * ld * (1.0 - sig)
    d_au = d_alpha * alpha * (1.0 - alpha)
    d_vg = d_mv * (fv - vr)
    d_vu = d_vg * vg * (1.0 - vg)
    dr_out[...] = d_r.astype(dr_out.dtype)
    dk_out[...] = d_kr.astype(dk_out.dtype)
    dv_out[...] = (d_mv * (1.0 - vg)).astype(dv_out.dtype)
    ddu_out[...] = d_du.astype(ddu_out.dtype)
    dau_out[...] = d_au.astype(dau_out.dtype)
    dvu_out[...] = d_vu.astype(dvu_out.dtype)
    dfv_out[...] = d_mv * vg
    gvec_ref[...] = jnp.zeros_like(gvec_ref)
    gvec_ref[0:1] = jnp.sum(d_du, axis=0, keepdims=True)
    gvec_ref[1:2] = jnp.sum(d_au, axis=0, keepdims=True)
    gvec_ref[2:3] = jnp.sum(d_vu, axis=0, keepdims=True)
    gvec_ref[3:4] = jnp.sum(d_raw * kr, axis=0, keepdims=True)
    gvec_ref[4:5] = jnp.sum(d_sk * kr * (alpha - 1.0), axis=0, keepdims=True)
    gvec_ref[5:6] = jnp.sum(d_extra * r * sk, axis=0, keepdims=True)


def merge_body(old_o_ref, old_t_ref, o_ref, t_ref, new_o_ref, new_t_ref):
    for pair in range(o_ref.shape[0]):
        both = jnp.concatenate([old_o_ref[pair], old_t_ref[pair]], axis=0)
        moved = mm(both, spread(t_ref[pair]))
        new_o_ref[pair] = o_ref[pair] + moved[:HEAD]
        new_t_ref[pair] = moved[HEAD:].astype(new_t_ref.dtype)


def merge_last_body(old_o_ref, o_ref, t_ref, new_o_ref):
    for pair in range(o_ref.shape[0]):
        new_o_ref[pair] = o_ref[pair] + mm(old_o_ref[pair], spread(t_ref[pair]))


def merge_back_body(next_g_ref, g_ref, t_ref, new_g_ref):
    for pair in range(g_ref.shape[0]):
        new_g_ref[pair] = g_ref[pair] + mm(next_g_ref[pair], spread(t_ref[pair]), NT)


def cols(span):
    return pl.BlockSpec((span, PAIR), lambda pair: (0, pair))


def per_pair(rows):
    return pl.BlockSpec((1, rows, PAIR), lambda pair: (pair, 0, 0))


def fixed(shape):
    return pl.BlockSpec(shape, lambda pair: (0,) * len(shape))


def shaped(shape, dtype):
    return jax.ShapeDtypeStruct(shape, dtype)


def forward_call(raws, fv, vec, seg_col, seg_row):
    span, width = fv.shape
    pairs = width // PAIR
    return pl.pallas_call(
        forward_body,
        grid=(pairs,),
        in_specs=[cols(span)] * 7 + [cols(vec.shape[0]), fixed(seg_col.shape), fixed(seg_row.shape)],
        out_specs=[cols(span)] * 5 + [per_pair(2 * span), per_pair(HEAD), per_pair(HEAD)],
        out_shape=[
            shaped((span, width), BF16),
            shaped((span, width), BF16),
            shaped((span, width), F32),
            shaped((span, width), F32),
            shaped((span, width), F32),
            shaped((pairs, 2 * span, span), BF16),
            shaped((pairs, HEAD, PAIR), F32),
            shaped((pairs, HEAD, PAIR), F32),
        ],
        name="wkv_forward",
    )(*raws, fv, vec, seg_col, seg_row)


def finish_call(q, out, bonus, state, gate, vec):
    span, width = out.shape
    return pl.pallas_call(
        finish_body,
        grid=(width // PAIR,),
        in_specs=[cols(span)] * 3 + [per_pair(HEAD), cols(span), cols(vec.shape[0])],
        out_specs=[cols(span)] * 3,
        out_shape=[
            shaped((span, width), F32), shaped((span, width), F32), shaped((span, width), BF16),
        ],
        name="wkv_finish",
    )(q, out, bonus, state, gate, vec)


def early_call(d_branch, gate, xhat, rstd, bonus, q, vec):
    span, width = xhat.shape
    pairs = width // PAIR
    return pl.pallas_call(
        early_body,
        grid=(pairs,),
        in_specs=[cols(span)] * 6 + [cols(vec.shape[0])],
        out_specs=[cols(span)] * 3 + [per_pair(HEAD), cols(8)],
        out_shape=[
            shaped((span, width), F32),
            shaped((span, width), F32),
            shaped((span, width), BF16),
            shaped((pairs, HEAD, PAIR), F32),
            shaped((8, width), F32),
        ],
        name="wkv_early",
    )(d_branch, gate, xhat, rstd, bonus, q, vec)


def late_call(raws, fv, vec, seg_col, seg_row, x, y, u0, state, grad, dout, dbg):
    span, width = fv.shape
    pairs = width // PAIR
    return pl.pallas_call(
        late_body,
        grid=(pairs,),
        in_specs=[cols(span)] * 7
        + [cols(vec.shape[0]), fixed(seg_col.shape), fixed(seg_row.shape)]
        + [per_pair(2 * span), cols(span), cols(span), per_pair(HEAD), per_pair(HEAD)]
        + [cols(span)] * 2,
        out_specs=[cols(span)] * 7 + [cols(8)],
        out_shape=[shaped((span, width), BF16)] * 6
        + [shaped((span, width), F32), shaped((8, width), F32)],
        name="wkv_late",
    )(*raws, fv, vec, seg_col, seg_row, x, y, u0, state, grad, dout, dbg)


def merge_call(old_o, old_t, o, t):
    return pl.pallas_call(
        merge_body,
        out_shape=[shaped(o.shape, F32), shaped(o.shape, BF16)],
        name="state_merge",
    )(old_o, old_t, o, t)


def merge_last_call(old_o, o, t):
    return pl.pallas_call(
        merge_last_body, out_shape=shaped(o.shape, F32), name="state_merge_last"
    )(old_o, o, t)


def merge_back_call(next_g, g, t):
    return pl.pallas_call(
        merge_back_body, out_shape=shaped(g.shape, F32), name="state_merge_back"
    )(next_g, g, t)


def matmul(left, right):
    return jnp.dot(left, right, preferred_element_type=F32)


def matmul_nt(left, right):
    return lax.dot_general(left, right, NT, preferred_element_type=F32)


def matmul_tn(left, right):
    return lax.dot_general(left, right, TN, preferred_element_type=F32)


def layer_norm(values, gain, bias_row):
    center = values - jnp.mean(values, axis=-1, keepdims=True)
    spread_sq = jnp.mean(center * center, axis=-1, keepdims=True)
    return center * lax.rsqrt(spread_sq + LN_EPS) * gain + bias_row


def blend_rows(current, earlier, keep_row, gain_rows):
    change = earlier * keep_row - current
    return current[None] + change[None] * gain_rows[:, None, :]


def shifted(value, steps):
    count = lax.axis_size("seq")
    initial, last = (max(0, -steps), min(count, count - steps))
    return lax.ppermute(value, "seq", [(place, place + steps) for place in range(initial, last)])


def partner(value, axis, flip):
    count = lax.axis_size(axis)
    return lax.ppermute(value, axis, [(place, place ^ flip) for place in range(count)])


def after(value, *others):
    return lax.optimization_barrier((value,) + others)[0]


def gather_blocks(shard):
    count = lax.axis_size("fsdp")
    copies = jnp.broadcast_to(shard[None], (count,) + shard.shape)
    return lax.all_to_all(copies, "fsdp", split_axis=0, concat_axis=0, tiled=True)


def gather_weight(shard, axis, core):
    size = shard.shape[axis] // 2
    half = lax.dynamic_slice_in_dim(shard, core * size, size, axis)
    mine = gather_blocks(half)
    other = partner(mine, "seq", 1)
    low = jnp.where(core == 0, mine, other)
    high = jnp.where(core == 0, other, mine)
    return jnp.concatenate([low, high], axis=axis + 1)


def gather_rows(rows):
    count = lax.axis_size("fsdp")
    pieces = [rows] + [partner(rows, "fsdp", flip) for flip in range(1, count)]
    return jnp.concatenate(pieces, axis=0)


def scatter_rows(rows):
    count = lax.axis_size("fsdp")
    size = rows.shape[0] // count
    total = rows[:size].astype(F32)
    for flip in range(1, count):
        total = total + partner(rows[flip * size : (flip + 1) * size], "fsdp", flip).astype(F32)
    return total


def columns_to_owner(array):
    return lax.all_to_all(array, "fsdp", split_axis=array.ndim - 1, concat_axis=array.ndim - 2, tiled=True)


def reduce_seq(array):
    count = lax.axis_size("seq")
    chips = count // 2
    place = lax.axis_index("seq")
    core = place % 2
    chip = place // 2
    half = array.shape[0] // 2
    part = half // chips
    own = lax.dynamic_slice_in_dim(array, core * half, half, 0)
    other = partner(lax.dynamic_slice_in_dim(array, (1 - core) * half, half, 0), "seq", 1)
    on_chip = (own.astype(F32) + other.astype(F32)).astype(BF16).reshape(chips, part, -1)
    total = lax.dynamic_index_in_dim(on_chip, chip, 0, False).astype(F32)
    for flip in range(1, chips):
        leaving = lax.dynamic_index_in_dim(on_chip, chip ^ flip, 0, False)
        total = total + partner(leaving, "seq", 2 * flip).astype(F32)
    total = total.astype(BF16)
    pieces = jnp.zeros(on_chip.shape, BF16)
    pieces = lax.dynamic_update_index_in_dim(pieces, total, chip, 0)
    for flip in range(1, chips):
        pieces = lax.dynamic_update_index_in_dim(
            pieces, partner(total, "seq", 2 * flip), chip ^ flip, 0
        )
    mine = pieces.reshape(half, -1)
    other = partner(mine, "seq", 1)
    low = jnp.where(core == 0, mine, other)
    high = jnp.where(core == 0, other, mine)
    return jnp.concatenate([low, high], axis=0).astype(F32)


def by_core(core, mine, other):
    return (jnp.where(core == 0, mine, other), jnp.where(core == 0, other, mine))


def own_pairs(core, array):
    size = array.shape[0] // 2
    return lax.dynamic_slice_in_dim(array, core * size, size, 0)


def all_pairs(core, mine):
    low, high = by_core(core, mine, partner(mine, "seq", 1))
    return jnp.concatenate([low, high], axis=0)


def body(
    layer_input,
    first_layer_values,
    document_numbers,
    output_cotangent,
    projection_matrices,
    time_output_matrix,
    lowrank_first,
    lowrank_second,
    channel_key_matrix,
    channel_value_matrix,
    vectors,
):
    groups = lax.axis_size("fsdp")
    place = lax.axis_index("seq")
    core = place % 2
    chips = lax.axis_size("seq") // 2
    span, width = layer_input.shape[1:]
    resid_in = layer_input[0].astype(F32)
    first_values = first_layer_values[0]
    cotangent = output_cotangent[0]
    id_plus = document_numbers[0].astype(F32) + 1.0

    edge = jnp.concatenate(
        [resid_in[span - 1 :], jnp.broadcast_to(id_plus[span - 1 :, None], (1, PAIR))], axis=1
    )
    edge = shifted(edge, 1)
    vec_blocks = gather_blocks(vectors)
    down_blocks = gather_weight(lowrank_first, 0, core)
    second_blocks = gather_weight(lowrank_second, 0, core)
    proj_blocks = gather_weight(after(projection_matrices, down_blocks, second_blocks), 1, core)
    out_blocks = gather_weight(after(time_output_matrix, proj_blocks), 0, core)
    cot_rows = gather_rows(after(cotangent, out_blocks))

    vec = jnp.swapaxes(vec_blocks, 0, 1).reshape(-1, width).astype(F32)
    down = down_blocks.reshape(width, -1)
    second = jnp.swapaxes(second_blocks, 0, 1).reshape(-1, width)
    out_full = out_blocks.reshape(width, width)
    down_parts = [down[:, BOUNDS[part] : BOUNDS[part + 1]] for part in range(4)]
    second_parts = [second[BOUNDS[part] : BOUNDS[part + 1]] for part in range(4)]
    vec_rows = jnp.concatenate([vec, jnp.zeros((24 - vec.shape[0], width), F32)], axis=0)

    edge_id = edge[0, width]
    earlier_ids = jnp.concatenate([edge[0, width : width + 1], id_plus[:-1]])
    keep_row = (id_plus == earlier_ids).astype(F32)[:, None]
    segment = id_plus - edge_id
    seg_col = jnp.broadcast_to(segment[:, None], (span, PAIR))
    seg_row = jnp.broadcast_to(segment[None], (8, span))

    def mixer(current, earlier, gain_rows):
        return blend_rows(current, earlier, keep_row, gain_rows)

    normed_one, ln_one_back = jax.vjp(layer_norm, resid_in, vec[14], vec[15])
    edge_row = layer_norm(edge[:, :width], vec[14], vec[15])
    earlier_one = jnp.concatenate([edge_row, normed_one[:-1]])
    mixed_rows, mix_back = jax.vjp(mixer, normed_one, earlier_one, vec[0:6])
    mixed = mixed_rows.astype(BF16)
    decay_pre = matmul(mixed[1], down_parts[0])
    low_decay = jnp.tanh(decay_pre).astype(BF16)
    low_alpha = matmul(mixed[4], down_parts[1]).astype(BF16)
    low_vmix = matmul(mixed[3], down_parts[2]).astype(BF16)
    gate_pre = matmul(mixed[5], down_parts[3])
    low_gate = jax.nn.sigmoid(gate_pre).astype(BF16)
    lows = (low_decay, low_alpha, low_vmix, low_gate)
    decay_up, alpha_up, vmix_up, gate = [
        matmul(lows[part], second_parts[part]) for part in range(4)
    ]
    mix_three = (mixed[0], mixed[2], mixed[3])
    recept, key_raw, value_raw = [
        jnp.concatenate(
            [matmul(mix_three[part], proj_blocks[block, part]) for block in range(groups)], axis=1
        )
        for part in range(3)
    ]
    raws = (recept, key_raw, value_raw, decay_up, alpha_up, vmix_up)
    query, y_part, u_part, out_part, bonus, inverse, transfer, offset = forward_call(
        raws, first_values, vec_rows, seg_col, seg_row
    )
    mix_rows = lax.all_gather(
        after(jnp.stack(mix_three), cot_rows), "fsdp", axis=1, tiled=True
    )

    transfer_b = transfer.astype(BF16)
    both = jnp.concatenate([offset.astype(BF16), transfer_b], axis=0)
    other = partner(both, "seq", 1)
    pairs = offset.shape[0]
    other_offset, other_transfer = (other[:pairs], other[pairs:])
    offset_zero, offset_one = by_core(core, offset, other_offset.astype(F32))
    transfer_zero, transfer_one = by_core(core, transfer_b, other_transfer)
    chip_offset, chip_transfer = merge_call(
        own_pairs(core, offset_zero),
        own_pairs(core, transfer_zero),
        own_pairs(core, offset_one),
        own_pairs(core, transfer_one),
    )
    arriving = shifted(chip_offset.astype(BF16), 2)
    for _ in range(chips - 2):
        arriving = shifted(
            merge_last_call(arriving, chip_offset, chip_transfer).astype(BF16), 2
        )
    chip_state = all_pairs(core, arriving).astype(F32)
    state = jnp.where(
        core == 0, chip_state, merge_last_call(chip_state, offset_zero, transfer_zero)
    )

    xhat, rstd, branch = finish_call(query, out_part, bonus, state, gate, vec_rows)
    middle = resid_in + matmul(branch, out_full)
    normed_two, ln_two_back = jax.vjp(layer_norm, middle, vec[16], vec[17])
    edge_two = shifted(normed_two[span - 1 :], 1)
    earlier_two = jnp.concatenate([edge_two, normed_two[:-1]])
    cmix_in, cmix_back = jax.vjp(mixer, normed_two, earlier_two, vec[18:19])
    cmix_rows = gather_rows(cmix_in[0].astype(BF16))
    pre_act = matmul(cmix_rows, channel_key_matrix)
    d_hidden = matmul_nt(cot_rows, channel_value_matrix)
    active = jax.nn.relu(pre_act)
    hidden = jnp.square(active).astype(BF16)
    d_pre = (d_hidden * 2.0 * active).astype(BF16)
    d_cmix = scatter_rows(matmul_nt(d_pre, channel_key_matrix).astype(BF16))
    block_out = (
        middle + scatter_rows(after(matmul(hidden, channel_value_matrix).astype(BF16), d_cmix))
    ).astype(BF16)
    grad_value = matmul_tn(hidden, cot_rows)
    grad_key = matmul_tn(cmix_rows, d_pre)
    grad_value, grad_key = [
        part.astype(F32)
        for part in lax.psum((grad_value.astype(BF16), grad_key.astype(BF16)), "seq")
    ]

    d_normed_two, d_earlier_two, d_cmix_gain = cmix_back(d_cmix[None])
    back_two = shifted(d_earlier_two[:1], -1)
    d_middle, d_gain_two, d_bias_two = ln_two_back(
        d_normed_two + jnp.concatenate([d_earlier_two[1:], back_two])
    )
    d_middle = d_middle + cotangent.astype(F32)
    d_middle_b = d_middle.astype(BF16)
    d_branch = matmul_nt(d_middle_b, out_full)
    d_out, d_inner, d_gate, start_grad, vec_early = early_call(
        d_branch, gate, xhat, rstd, bonus, query, vec_rows
    )

    other_start = partner(start_grad.astype(BF16), "seq", 1).astype(F32)
    start_zero, start_one = by_core(core, start_grad, other_start)
    chip_start = merge_back_call(
        own_pairs(core, start_one), own_pairs(core, start_zero), own_pairs(core, transfer_zero)
    )
    arriving = shifted(chip_start.astype(BF16), -2)
    for _ in range(chips - 2):
        arriving = shifted(
            merge_back_call(arriving, chip_start, chip_transfer).astype(BF16), -2
        )
    chip_end = all_pairs(core, arriving).astype(F32)
    end_grad = jnp.where(
        core == 0, merge_back_call(chip_end, start_one, transfer_one), chip_end
    )

    d_recept, d_key, d_value, d_decay, d_alpha, d_vmix, d_first, vec_late = late_call(
        raws, first_values, vec_rows, seg_col, seg_row,
        inverse, y_part, u_part, state, end_grad, d_out, d_inner,
    )

    branch_cols = columns_to_owner(after(branch, d_cmix))
    d_middle_rows = lax.all_gather(d_middle_b, "fsdp", axis=0, tiled=True)
    grad_out = reduce_seq(matmul_tn(branch_cols, d_middle_rows).astype(BF16))

    head_grads = columns_to_owner(jnp.stack([d_recept, d_key, d_value]))
    grad_proj = jnp.concatenate(
        [matmul_tn(mix_rows[part], head_grads[part]) for part in range(3)], axis=0
    ).astype(BF16)

    ups = (d_decay, d_alpha, d_vmix, d_gate)
    grad_up = jnp.concatenate([matmul_tn(lows[part], ups[part]) for part in range(4)], axis=0)
    d_lows = [matmul_nt(ups[part], second_parts[part]) for part in range(4)]
    tanh_now = jnp.tanh(decay_pre)
    sigma_now = jax.nn.sigmoid(gate_pre)
    low_grads = (
        (d_lows[0] * (1.0 - tanh_now * tanh_now)).astype(BF16),
        d_lows[1].astype(BF16),
        d_lows[2].astype(BF16),
        (d_lows[3] * sigma_now * (1.0 - sigma_now)).astype(BF16),
    )
    low_mixes = (mixed[1], mixed[4], mixed[3], mixed[5])
    grad_down = jnp.concatenate(
        [matmul_tn(low_grads[part], low_mixes[part]) for part in range(4)], axis=0
    )
    wide = jnp.moveaxis(proj_blocks, 0, 2).reshape(3, width, width)
    d_mixed = jnp.stack(
        [
            matmul_nt(d_recept, wide[0]),
            matmul_nt(low_grads[0], down_parts[0]),
            matmul_nt(d_key, wide[1]),
            matmul_nt(d_value, wide[2]) + matmul_nt(low_grads[2], down_parts[2]),
            matmul_nt(low_grads[1], down_parts[1]),
            matmul_nt(low_grads[3], down_parts[3]),
        ]
    )
    d_normed_one, d_earlier_one, d_mix_gains = mix_back(d_mixed)
    back_one = shifted(d_earlier_one[:1], -1)
    d_resid, d_gain_one, d_bias_one = ln_one_back(
        d_normed_one + jnp.concatenate([d_earlier_one[1:], back_one])
    )
    d_input = d_resid + d_middle

    grad_vec = jnp.concatenate(
        [
            d_mix_gains,
            vec_late[0:6],
            vec_early[4:6],
            d_gain_one[None],
            d_bias_one[None],
            d_gain_two[None],
            d_bias_two[None],
            d_cmix_gain,
        ],
        axis=0,
    )
    small = jnp.concatenate([grad_up, grad_down, grad_vec], axis=0).astype(BF16)
    block = 2 * 16 * chips
    rows = 3 * width + small.shape[0]
    fill = -rows % block
    small = jnp.concatenate([small, jnp.zeros((fill, width), BF16)], axis=0)
    small_cols = columns_to_owner(small[:, None]).astype(F32)
    small_own = jnp.sum(small_cols, axis=1).astype(BF16)
    total = reduce_seq(jnp.concatenate([grad_proj, small_own], axis=0))
    base = 3 * width
    inner = BOUNDS[4]
    return (
        block_out[None],
        d_input[None],
        d_first[None],
        total[:base].reshape(3, width, -1),
        grad_out,
        total[base + inner : base + 2 * inner].T,
        total[base : base + inner],
        grad_key,
        grad_value,
        total[base + 2 * inner : base + 2 * inner + vectors.shape[0]],
    )


def solution(mesh):
    in_specs = (
        P("fsdp", "seq", None),
        P("fsdp", "seq", None),
        P("fsdp", "seq"),
        P("fsdp", "seq", None),
        P(None, None, "fsdp"),
        P("fsdp", None),
        P("fsdp", None),
        P(None, "fsdp"),
        P(None, "fsdp"),
        P("fsdp", None),
        P(None, "fsdp"),
    )
    out_specs = (
        P("fsdp", "seq", None),
        P("fsdp", "seq", None),
        P("fsdp", "seq", None),
        P(None, None, "fsdp"),
        P("fsdp", None),
        P("fsdp", None),
        P(None, "fsdp"),
        P(None, "fsdp"),
        P("fsdp", None),
        P(None, "fsdp"),
    )
    return jax.shard_map(body, mesh=mesh, in_specs=in_specs, out_specs=out_specs, check_vma=False)
```

time: 1200 us -> 633 us (0.53)
  other arithmetic: 258 us -> 82.2 us
  matrix products: 225 us -> 55.9 us
  waiting for transfers between devices: 369 us -> 206 us
  blocking collectives: 96.4 us -> 0 us
  Pallas kernels: 0 us -> 78.1 us
  local copies, waits for them, and re-layouts: 140 us -> 79.2 us
  starting transfers between devices: 82.7 us -> 101 us
    another operation x20 -> x2, other arithmetic: 170 us -> 1.04 us  [the longest x1 0.95 us: body(): jnp.stack(mix_three)]
    dot_general x194 -> x51, matrix products: 219 us -> 55.9 us  [the longest x14 24.4 us: matmul_tn(): return lax.dot_general(left, right, TN, preferred_element_type=F32)]
    reduce_scatter x5 -> x0, waiting for transfers between devices: 119 us -> none  [the longest x1 34.5 us: body(): lax.psum_scatter(matmul(branch_b, time_output_matrix).astype(jnp.bfloat16...]
    pallas_call x0 -> x12, Pallas kernels: none -> 78.1 us  [the longest x1 33 us: forward_call(): pl.pallas_call(forward_body, grid=(pairs,), in_specs=[cols(span)] * 7 + [...]
    all_gather x5 -> x0, blocking collectives: 67.1 us -> none  [the longest x1 21 us: body(): lax.all_gather(lowrank_first, 'fsdp', axis=0, tiled=True)]
    all_gather x6 -> x2, waiting for transfers between devices: 57.1 us -> 0.02 us  [the longest x1 0.02 us: body(): lax.all_gather(after(jnp.stack(mix_three), cot_rows), 'fsdp', axis=1, til...]
    psum x1, waiting for transfers between devices: 116 us -> 69.3 us  [body(): lax.psum((grad_value.astype(BF16), grad_key.astype(BF16)), 'seq')]
    ppermute x19 -> x46, waiting for transfers between devices: 56.2 us -> 100 us  [the longest x36 89.3 us: partner(): lax.ppermute(value, axis, [(place, place ^ flip) for place in range(count)])]
  transfers between devices with their start and end apart: 33 -> 57, of which waited for: 27 -> 22; matrix products, arithmetic and copies ran while one was open for 23% -> 33% of each run, Pallas kernels for 0% -> 13%
where the time goes in v1:
time: 633 us; the launch traced here: 621 us
  waiting for transfers between devices  206 us (33%)
  starting transfers between devices  101 us (16%)
  other arithmetic  82.2 us (13%)
  local copies, waits for them, and re-layouts  79.2 us (13%)
  Pallas kernels  78.1 us (12%)
  matrix products  55.9 us (9%)
  between operations  19 us (3%)
    ppermute x36, waiting for transfers between devices, partner(): lax.ppermute(value, axis, [(place, place ^ flip) for place in range(count)])  89.3 us
    psum x1, waiting for transfers between devices, body(): lax.psum((grad_value.astype(BF16), grad_key.astype(BF16)), 'seq')  69.3 us
    ppermute x36, starting transfers between devices, partner(): lax.ppermute(value, axis, [(place, place ^ flip) for place in range(count)])  43.3 us
    pallas_call x1, Pallas kernels, forward_call(): pl.pallas_call(forward_body, grid=(pairs,), in_specs=[cols(span)] * 7 + [...  33 us
    all_to_all x5, waiting for transfers between devices, gather_blocks(): lax.all_to_all(copies, 'fsdp', split_axis=0, concat_axis=0, tiled=True)  29.8 us
    dot_general x14, matrix products, matmul_tn(): return lax.dot_general(left, right, TN, preferred_element_type=F32)  24.4 us
    ppermute x10, starting transfers between devices, shifted(): lax.ppermute(value, 'seq', [(place, place + steps) for place in range(ini...  23.1 us
    all_to_all x5, starting transfers between devices, gather_blocks(): lax.all_to_all(copies, 'fsdp', split_axis=0, concat_axis=0, tiled=True)  21.6 us
  transfers between devices with their start and end apart: 57, of which 22 were waited for; matrix products, arithmetic and copies ran while one was open for 33% of the time, Pallas kernels for 13%

profile of v1, /device:TPU:0, one launch (start us, length us, event | category | flops | bytes accessed | tf_op | source)
XLA Modules:
  0.0 621.0 jit_solution(6213316178563741149)
XLA Ops:
  9.8 5.2 all-to-all-start.2
  35.8 4.8 all-to-all-start.3
  50.1 27.6 %all-to-all-done.3 = bf16[4,3,512,256]{2,3,1,0:T(8,128)(2,1)} async-done(((bf16[4,3,512,256]{2,3,1,0:T(8,128)(2,1)}), bf16[4,3,512,256]{2,3,1,0:T(8,128)(2,1)}, u32[]{:S(2)}, u32[]{:S(2)}) %all-to-all-start.3) | async-done | bytes 3145760 | tf_op jit(solution)/shard_map/all_to_all | solution.py:527
  114.6 33.0 %wkv_forward.1 = (bf16[128,1024]{1,0:T(8,128)(2,1)}, bf16[128,1024]{1,0:T(8,128)(2,1)}, f32[128,1024]{1,0:T(8,128)}, f32[128,1024]{1,0:T(8,128)}, f32[128,1024]{...) custom-call(f32[128,1024]{1,0:T(8,128)} %get-tuple-element.158.r_ref, ...), custom_call_target="tpu_custom_call" | custom-call | tf_op jit(solution)/shard_map/wkv_forward/pallas_call | solution.py:397
  191.5 7.2 %wkv_finish.1 = (f32[128,1024]{1,0:T(8,128)}, f32[128,1024]{1,0:T(8,128)}, bf16[128,1024]{1,0:T(8,128)(2,1)}) custom-call(bf16[128,1024]{1,0:T(8,128)(2,1)} %get-tuple-element.43.q_ref, f32[128,1024]{1,0:T(8,128)} %get-tuple-element.44.out_ref, f32[128,1024]{1,0:T(8,128)} %get-tuple-element.45.bonus_ref, f32[8,64,128]{2,1,0:T(8,128)} %broadcast_select_fusion.13.s_ref, ...), custom_call_target="tpu_custom_call" | custom-call | tf_op jit(solution)/shard_map/wkv_finish/pallas_call | solution.py:418
  214.0 7.1 %collective-permute-done.15 = bf16[128,1024]{1,0:T(8,128)(2,1)S(1)} collective-permute-done((bf16[128,1024]{1,0:T(8,128)(2,1)}, bf16[128,1024]{1,0:T(8,128)(2,1)S(1)}, u32[]{:S(2)}, u32[]{:S(2)}) %collective-permute-start.15) | collective-permute-done | bytes 262176 | tf_op jit(solution)/shard_map/ppermute | solution.py:517
  222.7 9.7 %collective-permute-done.12 = bf16[128,1024]{1,0:T(8,128)(2,1)} collective-permute-done((bf16[128,1024]{1,0:T(8,128)(2,1)}, bf16[128,1024]{1,0:T(8,128)(2,1)}, u32[]{:S(2)}, u32[]{:S(2)}) %collective-permute-start.12) | collective-permute-done | bytes 262176 | tf_op jit(solution)/shard_map/ppermute | solution.py:517
  249.0 6.0 collective-permute-done.19
  262.3 10.1 %collective-permute-done.20 = bf16[128,1024]{1,0:T(8,128)(2,1)S(1)} collective-permute-done((bf16[128,1024]{1,0:T(8,128)(2,1)S(1)}, bf16[128,1024]{1,0:T(8,128)(2,1)S(1)}, u32[]{:S(2)}, u32[]{:S(2)}) %collective-permute-start.20) | collective-permute-done | bytes 262176 | tf_op jit(solution)/shard_map/ppermute | solution.py:517
  275.7 7.1 %collective-permute-done.22 = bf16[128,1024]{1,0:T(8,128)(2,1)S(1)} collective-permute-done((bf16[128,1024]{1,0:T(8,128)(2,1)S(1)}, bf16[128,1024]{1,0:T(8,128)(2,1)S(1)}, u32[]{:S(2)}, u32[]{:S(2)}) %collective-permute-start.22) | collective-permute-done | bytes 262176 | tf_op jit(solution)/shard_map/ppermute | solution.py:517
  288.0 6.9 %wkv_early.1 = (f32[128,1024]{1,0:T(8,128)}, f32[128,1024]{1,0:T(8,128)}, bf16[128,1024]{1,0:T(8,128)(2,1)}, f32[8,64,128]{2,1,0:T(8,128)}, f32[8,1024]{1,0:T(8,128)}) custom-call(f32[128,1024]{1,0:T(8,128)} %fusion.129.db_ref, f32[128,1024]{1,0:T(8,128)} %fusion.86.gate_ref, f32[128,1024]{1,0:T(8,128)} %get-tuple-element.57.xhat_ref, ...), custom_call_target="tpu_custom_call" | custom-call | tf_op jit(solution)/shard_map/wkv_early/pallas_call | solution.py:433
  296.1 5.4 fusion.115
  307.3 5.7 fusion.120
  319.2 5.4 collective-permute-done.26.next_g_ref
  341.0 16.2 %wkv_late.1 = (bf16[128,1024]{1,0:T(8,128)(2,1)}, bf16[128,1024]{1,0:T(8,128)(2,1)}, bf16[128,1024]{1,0:T(8,128)(2,1)}, bf16[128,1024]{1,0:T(8,128)(2,1)}, bf16[...) custom-call(f32[128,1024]{1,0:T(8,128)} %get-tuple-element.158.r_ref, ...), custom_call_target="tpu_custom_call" | custom-call | tf_op jit(solution)/shard_map/wkv_late/pallas_call | solution.py:452
  386.3 6.9 %concatenate.115 = bf16[595,1024]{1,0:T(8,128)(2,1)S(1)} concatenate(bf16[64,1024]{1,0:T(8,128)(2,1)} %convolution_convert_fusion.13, bf16[64,1024]{1,0:T(8,128)(2,1)S(1)} %convolution_convert_fusion.12, bf16[32,1024]{1,0:T(8,128)(2,1)S(1)} %copy-done.54, bf16[128,1024]{1,0:T(8,128)(2,1)S(1)} %convolution_convert_fusion.9, bf16[64,1024]{1,0:T(8,128)(2,1)} %convolution_convert_fusion.11, ...), dimensions={0} | concatenate | bytes 2437120 | tf_op jit(solution)/shard_map/concatenate | solution.py:817
  394.4 5.0 copy.80
  399.9 9.7 %reduce.14 = bf16[1024,640]{1,0:T(8,128)(2,1)} reduce(bf16[1024,1,640]{2,1,0:T(2,128)(2,1)S(1)} %bitcast.288, bf16[]{:T(256)} %broadcast.198), dimensions={1}, to_apply=%bitcast.228.reduce_sub_computation | reduce | bytes 2621442
  428.4 6.4 %all-to-all-done.6 = bf16[4,2,81920]{2,1,0:T(2,128)(2,1)S(1)} async-done(((bf16[4,2,81920]{2,1,0:T(2,128)(2,1)}), bf16[4,2,81920]{2,1,0:T(2,128)(2,1)S(1)}, u32[]{:S(2)}, u32[]{:S(2)}) %all-to-all-start.6) | async-done | bytes 1310752 | tf_op jit(solution)/shard_map/all_to_all | solution.py:556
  475.1 9.3 %collective-permute-done.32 = bf16[464,256]{1,0:T(8,128)(2,1)S(1)} collective-permute-done((bf16[464,256]{1,0:T(8,128)(2,1)S(1)}, bf16[464,256]{1,0:T(8,128)(2,1)S(1)}, u32[]{:S(2)}, u32[]{:S(2)}) %collective-permute-start.32) | collective-permute-done | bytes 237600 | tf_op jit(solution)/shard_map/ppermute | solution.py:517
  485.7 9.5 %collective-permute-start.34 = (bf16[464,256]{1,0:T(8,128)(2,1)S(1)}, bf16[464,256]{1,0:T(8,128)(2,1)S(1)}, u32[]{:S(2)}, u32[]{:S(2)}) collective-permute-start(bf16[464,256]{1,0:T(8,128)(2,1)S(1)} %get-tuple-element.88), channel_id=1, source_target_pairs={{0,2},{1,3},{2,0},{3,1},{4,6},{5,7},{6,4},{7,5},{8,10},{9,11},{10,... | collective-permute-start | bytes 712712 | tf_op jit(solution)/shard_map/ppermute | solution.py:517
  501.6 7.4 %collective-permute-done.34 = bf16[464,256]{1,0:T(8,128)(2,1)S(1)} collective-permute-done((bf16[464,256]{1,0:T(8,128)(2,1)S(1)}, bf16[464,256]{1,0:T(8,128)(2,1)S(1)}, u32[]{:S(2)}, u32[]{:S(2)}) %collective-permute-start.34) | collective-permute-done | bytes 237600 | tf_op jit(solution)/shard_map/ppermute | solution.py:517
  509.0 19.5 %collective-permute-done.35 = bf16[464,256]{1,0:T(8,128)(2,1)S(1)} collective-permute-done((bf16[464,256]{1,0:T(8,128)(2,1)S(1)}, bf16[464,256]{1,0:T(8,128)(2,1)S(1)}, u32[]{:S(2)}, u32[]{:S(2)}) %collective-permute-start.35) | collective-permute-done | bytes 237600 | tf_op jit(solution)/shard_map/ppermute | solution.py:517
  531.3 69.3 %all-reduce.6.cloned.1.call-done = (bf16[1024,1024]{1,0:T(8,128)(2,1)}, bf16[1024,1024]{1,0:T(8,128)(2,1)}) async-done(((bf16[1024,1024]{1,0:T(8,128)(2,1)}, bf16[1024,1024]{1,0:T(8,128)(2,1)}), (bf16[1024,1024]{1,0:T(8,128)(2,1)}, bf16[1024,1024]{1,0:T(8,128)(2,1)})) %all-reduce.6.cloned.1.call-update) | async-done | bytes 4194320 | tf_op jit(solution)/shard_map/psum | solution.py:727
  (521 shorter events, 301.8 us)
Async XLA Ops:
  18.0 25.4 %collective-permute-start = (f32[1,1152]{1,0:T(1,128)S(1)}, f32[1,1152]{1,0:T(1,128)S(1)}, u32[]{:S(2)}, u32[]{:S(2)}) collective-permute-start(f32[1,1152]{1,0:T(1,128)S(1)} %concatenate.93), channel_id=1, source_target_pairs={{0,1},{1,2},{2,3},{3,4},{4,5},{5,6},{6,7},{8,9},{9,10},{10,11},{11... | collective-permute-start | bytes 13832 | tf_op jit(solution)/shard_map/ppermute | solution.py:512
  35.8 41.8 %all-to-all-start.3 = ((bf16[4,3,512,256]{2,3,1,0:T(8,128)(2,1)}), bf16[4,3,512,256]{2,3,1,0:T(8,128)(2,1)}, u32[]{:S(2)}, u32[]{:S(2)}) async-start(bf16[4,3,512,256]{2,3,1,0:T(8,128)(2,1)} %broadcast_in_dim.138), calls=%async_computation.3 | async-start | bytes 6291456 | tf_op jit(solution)/shard_map/all_to_all | solution.py:527
  87.1 17.1 %collective-permute-start.3 = (bf16[4,3,512,256]{2,3,0,1:T(8,128)(2,1)}, bf16[4,3,512,256]{2,3,0,1:T(8,128)(2,1)}, u32[]{:S(2)}, u32[]{:S(2)}) collective-permute-start(bf16[4,3,512,256]{2,3,0,1:T(8,128)(2,1)} %copy.68), channel_id=1, source_target_pairs={{0,1},{1,0},{2,3},{3,2},{4,5},{5,4},{6,7},{7,6},{8,9},{9,8},{10,11... | collective-permute-start | bytes 9437192 | tf_op jit(solution)/shard_map/ppermute | solution.py:517
  91.1 60.7 %all-to-all-start.4 = ((bf16[4,128,1024]{2,1,0:T(8,128)(2,1)}), bf16[4,128,1024]{2,1,0:T(8,128)(2,1)}, u32[]{:S(2)}, u32[]{:S(2)}) async-start(bf16[4,128,1024]{2,1,0:T(8,128)(2,1)} %broadcast_in_dim.142), calls=%async_computation.4 | async-start | bytes 2097152 | tf_op jit(solution)/shard_map/all_to_all | solution.py:527
  95.3 325.5 %all-gather.3.cloned.1.call-start = ((), (), s32[]{:S(2)}) async-start(), calls=%async_computation.8 | async-start | bytes 3932160 | tf_op jit(solution)/shard_map/all_gather | solution.py:680
  151.7 31.1 %collective-permute-start.9 = (bf16[4,128,1024]{2,1,0:T(8,128)(2,1)}, bf16[4,128,1024]{2,1,0:T(8,128)(2,1)}, u32[]{:S(2)}, u32[]{:S(2)}) collective-permute-start(bf16[4,128,1024]{2,1,0:T(8,128)(2,1)} %all-to-all-done.4), channel_id=1, source_target_pairs={{0,1},{1,0},{2,3},{3,2},{4,5},{5,4},{6,7},{7,6},{8,9},{9,8},{10,11... | collective-permute-start | bytes 3145736 | tf_op jit(solution)/shard_map/ppermute | solution.py:517
  186.2 25.9 %collective-permute-start.14 = (bf16[128,1024]{1,0:T(8,128)(2,1)}, bf16[128,1024]{1,0:T(8,128)(2,1)}, u32[]{:S(2)}, u32[]{:S(2)}) collective-permute-start(bf16[128,1024]{1,0:T(8,128)(2,1)} %bitcast.46), channel_id=1, source_target_pairs={{0,8},{8,0},{16,24},{24,16},{1,9},{9,1},{17,25},{25,17},{2,10},{10... | collective-permute-start | bytes 786440 | tf_op jit(solution)/shard_map/ppermute | solution.py:517
  210.6 21.8 %collective-permute-start.12 = (bf16[128,1024]{1,0:T(8,128)(2,1)}, bf16[128,1024]{1,0:T(8,128)(2,1)}, u32[]{:S(2)}, u32[]{:S(2)}) collective-permute-start(bf16[128,1024]{1,0:T(8,128)(2,1)} %add_convert_fusion.4), channel_id=1, source_target_pairs={{0,16},{8,24},{16,0},{24,8},{1,17},{9,25},{17,1},{25,9},{2,18},{10... | collective-permute-start | bytes 786440 | tf_op jit(solution)/shard_map/ppermute | solution.py:517
  212.0 20.4 %collective-permute-start.13 = (bf16[128,1024]{1,0:T(8,128)(2,1)}, bf16[128,1024]{1,0:T(8,128)(2,1)}, u32[]{:S(2)}, u32[]{:S(2)}) collective-permute-start(bf16[128,1024]{1,0:T(8,128)(2,1)} %add_convert_fusion.4), channel_id=1, source_target_pairs={{0,24},{8,16},{16,8},{24,0},{1,25},{9,17},{17,9},{25,1},{2,26},{10... | collective-permute-start | bytes 786440 | tf_op jit(solution)/shard_map/ppermute | solution.py:517
  222.6 225.0 %all-gather.5.cloned.1.call-start = ((), (), s32[]{:S(2)}) async-start(), calls=%async_computation.9 | async-start | bytes 1310720 | tf_op jit(solution)/shard_map/all_gather | solution.py:763
  261.5 21.3 %collective-permute-start.22 = (bf16[128,1024]{1,0:T(8,128)(2,1)S(1)}, bf16[128,1024]{1,0:T(8,128)(2,1)S(1)}, u32[]{:S(2)}, u32[]{:S(2)}) collective-permute-start(bf16[128,1024]{1,0:T(8,128)(2,1)S(1)} %get-tuple-element.107), channel_id=1, source_target_pairs={{0,24},{8,16},{16,8},{24,0},{1,25},{9,17},{17,9},{25,1},{2,26},{10... | collective-permute-start | bytes 786440 | tf_op jit(solution)/shard_map/ppermute | solution.py:517
  377.7 35.5 %all-to-all-start.5 = ((bf16[3,128,1024]{1,0,2:T(4,128)(2,1)}), bf16[3,128,1024]{1,0,2:T(4,128)(2,1)}, u32[]{:S(2)}, u32[]{:S(2)}) async-start(bf16[3,128,1024]{1,0,2:T(4,128)(2,1)} %copy.75), calls=%async_computation.5 | async-start | bytes 2097152 | tf_op jit(solution)/shard_map/all_to_all | solution.py:556
  413.1 21.6 %all-to-all-start.6 = ((bf16[4,2,81920]{2,1,0:T(2,128)(2,1)}), bf16[4,2,81920]{2,1,0:T(2,128)(2,1)S(1)}, u32[]{:S(2)}, u32[]{:S(2)}) async-start(bf16[4,2,81920]{2,1,0:T(2,128)(2,1)} %reshape.367), calls=%async_computation.6 | async-start | bytes 2621440 | tf_op jit(solution)/shard_map/all_to_all | solution.py:556
  439.0 161.5 %all-reduce.6.cloned.1.call-start = ((), (), s32[]{:S(2)}) async-start(), calls=%async_computation.10 | async-start | bytes 8388608 | tf_op jit(solution)/shard_map/psum | solution.py:727
  462.6 21.8 %collective-permute-start.32 = (bf16[464,256]{1,0:T(8,128)(2,1)S(1)}, bf16[464,256]{1,0:T(8,128)(2,1)S(1)}, u32[]{:S(2)}, u32[]{:S(2)}) collective-permute-start(bf16[464,256]{1,0:T(8,128)(2,1)S(1)} %get-tuple-element.116), channel_id=1, source_target_pairs={{0,4},{1,5},{2,6},{3,7},{4,0},{5,1},{6,2},{7,3},{8,12},{9,13},{10,... | collective-permute-start | bytes 712712 | tf_op jit(solution)/shard_map/ppermute | solution.py:517
  464.5 19.9 %collective-permute-start.33 = (bf16[464,256]{1,0:T(8,128)(2,1)S(1)}, bf16[464,256]{1,0:T(8,128)(2,1)}, u32[]{:S(2)}, u32[]{:S(2)}) collective-permute-start(bf16[464,256]{1,0:T(8,128)(2,1)S(1)} %get-tuple-element.115), channel_id=1, source_target_pairs={{0,6},{1,7},{2,4},{3,5},{4,2},{5,3},{6,0},{7,1},{8,14},{9,15},{10,... | collective-permute-start | bytes 712712 | tf_op jit(solution)/shard_map/ppermute | solution.py:517
  471.5 29.2 %collective-permute-start.42 = (bf16[32,1024]{1,0:T(8,128)(2,1)S(1)}, bf16[32,1024]{1,0:T(8,128)(2,1)S(1)}, u32[]{:S(2)}, u32[]{:S(2)}) collective-permute-start(bf16[32,1024]{1,0:T(8,128)(2,1)S(1)} %get-tuple-element.86), channel_id=1, source_target_pairs={{0,2},{1,3},{2,0},{3,1},{4,6},{5,7},{6,4},{7,5},{8,10},{9,11},{10,... | collective-permute-start | bytes 196616 | tf_op jit(solution)/shard_map/ppermute | solution.py:517
  485.7 23.3 %collective-permute-start.34 = (bf16[464,256]{1,0:T(8,128)(2,1)S(1)}, bf16[464,256]{1,0:T(8,128)(2,1)S(1)}, u32[]{:S(2)}, u32[]{:S(2)}) collective-permute-start(bf16[464,256]{1,0:T(8,128)(2,1)S(1)} %get-tuple-element.88), channel_id=1, source_target_pairs={{0,2},{1,3},{2,0},{3,1},{4,6},{5,7},{6,4},{7,5},{8,10},{9,11},{10,... | collective-permute-start | bytes 712712 | tf_op jit(solution)/shard_map/ppermute | solution.py:517
  495.2 33.4 %collective-permute-start.43 = (bf16[32,1024]{1,0:T(8,128)(2,1)S(1)}, bf16[32,1024]{1,0:T(8,128)(2,1)S(1)}, u32[]{:S(2)}, u32[]{:S(2)}) collective-permute-start(bf16[32,1024]{1,0:T(8,128)(2,1)S(1)} %get-tuple-element.86), channel_id=1, source_target_pairs={{0,4},{1,5},{2,6},{3,7},{4,0},{5,1},{6,2},{7,3},{8,12},{9,13},{10,... | collective-permute-start | bytes 196616 | tf_op jit(solution)/shard_map/ppermute | solution.py:517
  497.3 31.4 %collective-permute-start.44 = (bf16[32,1024]{1,0:T(8,128)(2,1)S(1)}, bf16[32,1024]{1,0:T(8,128)(2,1)S(1)}, u32[]{:S(2)}, u32[]{:S(2)}) collective-permute-start(bf16[32,1024]{1,0:T(8,128)(2,1)S(1)} %get-tuple-element.86), channel_id=1, source_target_pairs={{0,6},{1,7},{2,4},{3,5},{4,2},{5,3},{6,0},{7,1},{8,14},{9,15},{10,... | collective-permute-start | bytes 196616 | tf_op jit(solution)/shard_map/ppermute | solution.py:517
  498.7 29.8 %collective-permute-start.35 = (bf16[464,256]{1,0:T(8,128)(2,1)S(1)}, bf16[464,256]{1,0:T(8,128)(2,1)S(1)}, u32[]{:S(2)}, u32[]{:S(2)}) collective-permute-start(bf16[464,256]{1,0:T(8,128)(2,1)S(1)} %get-tuple-element.88), channel_id=1, source_target_pairs={{0,4},{1,5},{2,6},{3,7},{4,0},{5,1},{6,2},{7,3},{8,12},{9,13},{10,... | collective-permute-start | bytes 712712 | tf_op jit(solution)/shard_map/ppermute | solution.py:517
  500.7 27.8 %collective-permute-start.36 = (bf16[464,256]{1,0:T(8,128)(2,1)S(1)}, bf16[464,256]{1,0:T(8,128)(2,1)S(1)}, u32[]{:S(2)}, u32[]{:S(2)}) collective-permute-start(bf16[464,256]{1,0:T(8,128)(2,1)S(1)} %get-tuple-element.88), channel_id=1, source_target_pairs={{0,6},{1,7},{2,4},{3,5},{4,2},{5,3},{6,0},{7,1},{8,14},{9,15},{10,... | collective-permute-start | bytes 712712 | tf_op jit(solution)/shard_map/ppermute | solution.py:517
  528.5 79.8 %collective-permute-start.37 = (bf16[1856,256]{1,0:T(8,128)(2,1)S(1)}, bf16[1856,256]{1,0:T(8,128)(2,1)}, u32[]{:S(2)}, u32[]{:S(2)}) collective-permute-start(bf16[1856,256]{1,0:T(8,128)(2,1)S(1)} %bitcast.298), channel_id=1, source_target_pairs={{0,1},{1,0},{2,3},{3,2},{4,5},{5,4},{6,7},{7,6},{8,9},{9,8},{10,11... | collective-permute-start | bytes 2850824 | tf_op jit(solution)/shard_map/ppermute | solution.py:517
  528.7 78.6 %collective-permute-start.45 = (bf16[128,1024]{1,0:T(8,128)(2,1)S(1)}, bf16[128,1024]{1,0:T(8,128)(2,1)S(1)}, u32[]{:S(2)}, u32[]{:S(2)}) collective-permute-start(bf16[128,1024]{1,0:T(8,128)(2,1)S(1)} %bitcast.319), channel_id=1, source_target_pairs={{0,1},{1,0},{2,3},{3,2},{4,5},{5,4},{6,7},{7,6},{8,9},{9,8},{10,11... | collective-permute-start | bytes 786440 | tf_op jit(solution)/shard_map/ppermute | solution.py:517
  (133 other events, 1452.3 us)
Sparse Core Ops, SparseCore 0:
  222.7 58.3 all-gather.2
  336.5 25.3 all-gather.4
Sparse Core Ops, SparseCore 1:
  469.9 130.6 all-reduce.5
